TPU v7x, 32 devices: a whole 2x2x4 slice. The times are simulated.
32 devices in a mesh: row: 8 (over z, x), col: 4 (over y, core).
Axes of the slice: x: 2, y: 2, z: 4, core: 2. Of those that a mesh axis runs over, the one named last changes fastest.
Arguments:
- off_blocks: bfloat16 [2048, 4, 96, 96], P(('row', 'col')), may hold values from -0.625 to 0.625
- neighbour: int32 [2048, 4], P(('row', 'col')), may hold values from 0 to 5
- active: int32 [2048, 4], P(('row', 'col')), may hold values 0 or 1
- diag_blocks: bfloat16 [2048, 96, 96], P(('row', 'col')), may hold values from -0.625 to 0.625
- diag_inverse: bfloat16 [2048, 96, 96], P(('row', 'col')), may hold values from -0.625 to 0.625
- tentative: bfloat16 [2048, 96, 96], P(('row', 'col')), may hold values from -0.21875 to 0.21875
- aggregate: int32 [2048], P(('row', 'col')), may hold values from 0 to 1
- owner_row: int32 [256, 1], P('row'), may hold values from 0 to 7; in each aligned block of 32 rows (0 to 31, 32 to 63, ...) at most 8 rows name the same one
- owner_group: int32 [256], P('row'), may hold values from 0 to 7
Outputs:
- coarse_blocks: float32 [64, 192, 192], P('row', 'col')
Inputs may be any that keep to these rules, and one draw needn't show every extreme that they name: `owner_row`: among the 32 clusters of one row tile at most 8 have the same owner row, and exactly 8 do in some tile.
All inputs are finite; a program needn't handle non-finite values. No bound on the sum of `active` on one device may be relied on, other than what follows from the above.
Results may differ from a plain program's by a relative error of at most 0.006.
Values may be sent and summed in bfloat16 or wider, within the bound.
No kernel may reach another device: no remote copies, remote signals or barrier semaphores. Data moves between devices by JAX's collectives and lax.ppermute only.
A program may use at most 128 MiB of HBM per device.

v0:
```python
import functools

import jax
import jax.numpy as jnp
from jax import lax
from jax.experimental import pallas as pl
from jax.experimental.pallas import tpu as pltpu
from jax.sharding import PartitionSpec as P


CW = 2
RQ = 2
G_DEV = 8
OMEGA = 0.6

EDGES = (0, 6, 10, 14, 16)
STEP = 2


VMEM = pl.BlockSpec(memory_space=pltpu.VMEM)
SMEM = pl.BlockSpec(memory_space=pltpu.SMEM)
ANY = pl.BlockSpec(memory_space=pl.ANY)
PARAMS = pltpu.CompilerParams(vmem_limit_bytes=25165824)
WIDE = pltpu.CompilerParams(vmem_limit_bytes=60817408)
ALONE = pltpu.CompilerParams(vmem_limit_bytes=67043328)


def step_of(first, count):
    return STEP if count % STEP == 0 and first % STEP == 0 else 1


def cost(flops, moved):
    return pl.CostEstimate(flops=int(flops), bytes_accessed=int(moved), transcendentals=0)


def pack_kernel(first, rows_ref, *outs):
    per = 2 * RQ
    width = rows_ref.shape[2]
    base = per * first
    for out in outs:
        for m in range(out.shape[0]):
            for j in range(per):
                out[m, :, j * width : (j + 1) * width] = rows_ref[base + per * m + j]
        base += per * out.shape[0]


def pack_rows(tentative, spans):
    per = 2 * RQ
    _, high, width = tentative.shape
    first, last = spans[0][0], spans[-1][1]
    whole = first % (last - first) == 0
    block = per * (last - first if whole else last)
    at = first // (last - first) if whole else 0
    counts = [stop - start for start, stop in spans]
    return pl.pallas_call(
        functools.partial(pack_kernel, 0 if whole else first),
        grid=(1,),
        in_specs=[pl.BlockSpec((block, high, width), lambda i: (at, 0, 0))],
        out_specs=[
            pl.BlockSpec((count, high, per * width), lambda i: (0, 0, 0)) for count in counts
        ],
        out_shape=[
            jax.ShapeDtypeStruct((count, high, per * width), tentative.dtype) for count in counts
        ],
        compiler_params=PARAMS if first else ALONE,
        cost_estimate=cost(0, 5 * sum(counts) * per * high * width),
    )(tentative)


def prolong_kernel(first, table, labels, off, diag, inverse, own, near_a, near_b, out, *wides):
    step = len(wides) // 2
    slots, size = off.shape[1], off.shape[2]
    window = CW * size
    base = pl.program_id(0) * step
    start = 2 * RQ * (first + base)

    @pl.when(pl.program_id(0) == 0)
    def _():
        for wide in wides:
            wide[3 * RQ] = jnp.zeros((size, window), wide.dtype)

    for c, wide in enumerate(wides):
        m = c // 2
        for k in range(RQ):
            local = RQ * c + k
            j = local % (2 * RQ)
            lanes = slice(j * size, (j + 1) * size)
            for side, block in enumerate(
                (near_a[base + m, :, lanes], own[local], near_b[base + m, :, lanes])
            ):
                label = labels[side, start + local]
                for w in range(CW):
                    wide[side * RQ + k, :, w * size : (w + 1) * size] = jnp.where(
                        label == w, block, jnp.zeros_like(block)
                    )
    sums = []
    for c, wide in enumerate(wides):
        for k in range(RQ):
            local = RQ * c + k
            total = jnp.dot(diag[local], wide[RQ + k], preferred_element_type=jnp.float32)
            for s in range(slots):
                total += jnp.dot(
                    off[local, s],
                    wide[table[s, start + local]],
                    preferred_element_type=jnp.float32,
                )
            sums.append(total.astype(out.dtype))
    for c, wide in enumerate(wides):
        for k in range(RQ):
            local = RQ * c + k
            change = jnp.dot(inverse[local], sums[local], preferred_element_type=jnp.float32)
            out[2 * base + c, :, k * window : (k + 1) * window] = (
                wide[RQ + k].astype(jnp.float32) - OMEGA * change
            ).astype(out.dtype)


def prolong_rows(table, labels, off, diag, inverse, tentative, near_a, near_b, first):
    per = 2 * RQ
    count = near_a.shape[0]
    slots, size = off.shape[1], off.shape[2]
    window = CW * size
    step = step_of(first, count)

    def rows(i):
        return (i + first // step, 0, 0)

    square = pl.BlockSpec((per * step, size, size), rows)
    return pl.pallas_call(
        functools.partial(prolong_kernel, first),
        grid=(count // step,),
        in_specs=[
            SMEM,
            SMEM,
            pl.BlockSpec((per * step, slots, size, size), lambda i: rows(i) + (0,)),
            square,
            square,
            square,
            VMEM,
            VMEM,
        ],
        out_specs=VMEM,
        out_shape=jax.ShapeDtypeStruct((2 * count, size, RQ * window), tentative.dtype),
        scratch_shapes=[pltpu.VMEM((3 * RQ + 1, size, window), tentative.dtype)] * (2 * step),
        compiler_params=PARAMS if first else WIDE,
        cost_estimate=cost(
            2 * count * per * (slots + 2) * size * size * window,
            2 * count * per * (slots + 7) * size * size,
        ),
    )(table, labels, off, diag, inverse, tentative, near_a, near_b)


def coarse_kernel(first, table, place, off, diag, own, near_a, near_b, keep, send, *scratch):
    step = len(scratch) // 6
    slots, size = off.shape[1], off.shape[2]
    window = CW * size
    halves, high = keep.shape[0], keep.shape[2]
    col = place[0]
    base = pl.program_id(0) * step
    start = 2 * RQ * (first + base)
    fields, stiffs, wholes = (scratch[2 * step * i : 2 * step * (i + 1)] for i in range(3))

    @pl.when(pl.program_id(0) == 0)
    def _():
        for field in fields:
            field[3 * RQ] = jnp.zeros((size, window), field.dtype)

    for c, field in enumerate(fields):
        for k in range(RQ):
            lanes = slice(k * window, (k + 1) * window)
            for side, source in enumerate((near_a, own, near_b)):
                field[side * RQ + k] = source[2 * base + c, :, lanes]
    for c, (field, stiff) in enumerate(zip(fields, stiffs)):
        for k in range(RQ):
            local = RQ * c + k
            total = jnp.dot(diag[local], field[RQ + k], preferred_element_type=jnp.float32)
            for s in range(slots):
                total += jnp.dot(
                    off[local, s],
                    field[table[s, start + local]],
                    preferred_element_type=jnp.float32,
                )
            stiff[k * size : (k + 1) * size, :] = total.astype(stiff.dtype)
    for field, stiff, whole in zip(fields, stiffs, wholes):
        left = field[RQ : 2 * RQ].reshape(RQ * size, window)
        block = lax.dot_general(
            left, stiff[...], (((0,), (0,)), ((), ())), preferred_element_type=jnp.float32
        )
        for piece in range(2 * halves):
            whole[piece] = block[piece * high : (piece + 1) * high]
    for c, whole in enumerate(wholes):
        lanes = slice(c % 2 * window, (c % 2 + 1) * window)
        for h in range(halves):
            keep[h, base + c // 2, :, lanes] = whole[col ^ (2 * h)]
            send[h, base + c // 2, :, lanes] = whole[col ^ (2 * h + 1)].astype(send.dtype)


def coarse_rows(table, place, off, diag, own, near_a, near_b, first, columns):
    per = 2 * RQ
    count = own.shape[0] // 2
    slots, size = off.shape[1], off.shape[2]
    window = CW * size
    halves, high = columns // 2, window // columns
    step = step_of(first, count)

    def rows(i):
        return (i + first // step, 0, 0)

    shape = (halves, count, high, 2 * window)
    return pl.pallas_call(
        functools.partial(coarse_kernel, first),
        grid=(count // step,),
        in_specs=[
            SMEM,
            SMEM,
            pl.BlockSpec((per * step, slots, size, size), lambda i: rows(i) + (0,)),
            pl.BlockSpec((per * step, size, size), rows),
            VMEM,
            VMEM,
            VMEM,
        ],
        out_specs=[VMEM, VMEM],
        out_shape=[
            jax.ShapeDtypeStruct(shape, jnp.float32),
            jax.ShapeDtypeStruct(shape, own.dtype),
        ],
        scratch_shapes=[pltpu.VMEM((3 * RQ + 1, size, window), own.dtype)] * (2 * step)
        + [pltpu.VMEM((RQ * size, window), own.dtype)] * (2 * step)
        + [pltpu.VMEM((columns, high, window), jnp.float32)] * (2 * step),
        compiler_params=PARAMS,
        cost_estimate=cost(
            2 * count * per * (slots + 3) * size * size * window,
            2 * count * per * (slots + 12) * size * size,
        ),
    )(table, place, off, diag, own, near_a, near_b)


def add_groups(targets, place, sides, first, sums):
    groups = sums.shape[0] - 1
    window = sums.shape[2]
    row = place[1]
    for side, source in enumerate(sides):

        def one(m, source=source, side=side):
            for u in range(2):
                target = targets[side, 2 * (first + m) + u]
                away = (target // G_DEV) ^ row
                spot = jnp.where(away % 2 == 0, away // 2 * G_DEV + target % G_DEV, groups)
                sums[spot] += source[m, :, u * window : (u + 1) * window].astype(jnp.float32)

        for m in range(source.shape[0]):
            one(m)


def bring(sources, buffers, sems):
    copies = [
        pltpu.make_async_copy(source, buffer, sems.at[i])
        for i, (source, buffer) in enumerate(zip(sources, buffers))
    ]
    for copy in copies:
        copy.start()
    return copies


def gather_kernel(starts, targets, place, *refs):
    count = 2 * len(starts)
    sources, sums, buffers, sems = refs[:count], refs[count], refs[count + 1 : -1], refs[-1]
    copies = bring(sources, buffers, sems)
    sums[...] = jnp.zeros_like(sums)
    for part, first in enumerate(starts):
        for copy in copies[2 * part : 2 * part + 2]:
            copy.wait()
        sides = [buffer.at[0] for buffer in buffers[2 * part : 2 * part + 2]]
        add_groups(targets, place, sides, first, sums)


def gather_groups(targets, place, parts, starts, rows):
    _, _, high, lanes = parts[0][0].shape
    shape = (rows // 2 * G_DEV + 1, high, lanes // 2)
    flat = [array for pair in parts for array in pair]
    total = sum(array.size for array in flat)
    return pl.pallas_call(
        functools.partial(gather_kernel, starts),
        in_specs=[SMEM, SMEM] + [ANY] * len(flat),
        out_specs=VMEM,
        out_shape=jax.ShapeDtypeStruct(shape, jnp.float32),
        scratch_shapes=[pltpu.VMEM(array.shape, array.dtype) for array in flat]
        + [pltpu.SemaphoreType.DMA((len(flat),))],
        compiler_params=PARAMS,
        cost_estimate=cost(total, 4 * total),
    )(targets, place, *flat)


def split_kernel(starts, begun, targets, place, *refs):
    count = 2 * len(starts)
    sources, (keep, odd, even, sums) = refs[: begun + count], refs[begun + count :][:4]
    buffers, sems = refs[begun + count + 4 : -1], refs[-1]
    copies = bring(sources, ((sums,) if begun else ()) + buffers, sems)
    window = sums.shape[2]
    for y in range(keep.shape[1]):
        if not begun:
            sums[...] = jnp.zeros_like(sums)
        if y == 0:
            for copy in copies:
                copy.wait()
        for part, first in enumerate(starts):
            sides = [buffer.at[y] for buffer in buffers[2 * part : 2 * part + 2]]
            add_groups(targets, place, sides, first, sums)
        for h in range(keep.shape[0]):
            send = odd if h % 2 else even
            for p in range(keep.shape[2]):
                for u in range(2):
                    lanes = slice(u * window, (u + 1) * window)
                    inner = 2 * p + u
                    keep[h, y, p, :, lanes] = sums[2 * h * G_DEV + inner]
                    away = sums[(2 * h + 1) * G_DEV + inner]
                    send[h // 2, y, p, :, lanes] = away.astype(send.dtype)


def split_groups(targets, place, early, parts, starts, rows):
    layers, _, high, lanes = parts[0][0].shape
    shape = (rows // 4, layers, G_DEV // 2, high, lanes)
    flat = [array for pair in parts for array in pair]
    half = jax.ShapeDtypeStruct((rows // 8,) + shape[1:], flat[0].dtype)
    sums = pltpu.VMEM((rows // 2 * G_DEV + 1, high, lanes // 2), jnp.float32)
    begun = [] if early is None else [early]
    assert layers == 1 or not begun
    return pl.pallas_call(
        functools.partial(split_kernel, starts, len(begun)),
        in_specs=[SMEM, SMEM] + [ANY] * (len(begun) + len(flat)),
        out_specs=[VMEM, VMEM, VMEM],
        out_shape=[jax.ShapeDtypeStruct(shape, jnp.float32), half, half],
        scratch_shapes=[sums]
        + [pltpu.VMEM(array.shape, array.dtype) for array in flat]
        + [pltpu.SemaphoreType.DMA((len(begun) + len(flat),))],
        compiler_params=PARAMS if rows <= 8 else ALONE,
        cost_estimate=cost(4 * rows * high * lanes, 100 * rows * high * lanes),
    )(targets, place, *begun, *flat)


def finish_kernel(*refs):
    terms, out_ref = refs[:-1], refs[-1]
    window = out_ref.shape[2]
    for p in range(out_ref.shape[0] // 2):
        total = sum(
            (term[0, 0, p] if term.ndim == 5 else term[0, p]).astype(jnp.float32) for term in terms
        )
        for u in range(2):
            out_ref[2 * p + u] = total[:, u * window : (u + 1) * window]


def finish(*terms):
    pairs, high, lanes = terms[0].shape[-3:]
    return pl.pallas_call(
        finish_kernel,
        in_specs=[VMEM] * len(terms),
        out_specs=VMEM,
        out_shape=jax.ShapeDtypeStruct((2 * pairs, high, lanes // 2), jnp.float32),
        compiler_params=PARAMS if len(terms[0]) <= 2 else ALONE,
        cost_estimate=cost(pairs * high * lanes, 10 * pairs * high * lanes),
    )(*terms)


def flip(count, bit):
    return [(i, i ^ bit) for i in range(count)]


def exchange(keep, send, axis, count, bit, link):
    terms = [(keep, 1)]
    while True:
        route = flip(count, bit)
        if isinstance(send, tuple):
            odd = lax.ppermute(send[0], axis, route)
            arrived = (lax.ppermute(send[1], axis, route), 1)
        else:
            arrived = (lax.ppermute(send, axis, route), 2)
            odd = arrived[0][1::2]
        bit *= 2
        if bit == count:
            return [term for term, _ in terms] + [arrived[0]]
        leave = sum(term[stride :: 2 * stride].astype(jnp.float32) for term, stride in terms)
        send = (leave + odd.astype(jnp.float32)).astype(link)
        terms = [(term, 2 * stride) for term, stride in terms] + [arrived]


def on_device(
    off_blocks,
    neighbour,
    active,
    diag_blocks,
    diag_inverse,
    tentative,
    aggregate,
    owner_row,
    owner_group,
):
    columns, rows = lax.axis_size("col"), lax.axis_size("row")
    col, row = lax.axis_index("col"), lax.axis_index("row")
    assert columns & (columns - 1) == 0 and columns >= 4
    assert rows & (rows - 1) == 0 and rows >= 8
    link = tentative.dtype
    groups = tentative.shape[0] // (2 * RQ)

    pair_a = flip(columns, 1)
    pair_b = [(i, (i + 1) % columns if i % 2 else (i - 1) % columns) for i in range(columns)]

    bounds = [groups * edge // EDGES[-1] for edge in EDGES]
    spans = list(zip(bounds[:-1], bounds[1:]))

    def both(block):
        near_b = lax.ppermute(block, "col", pair_b)
        near_a = lax.ppermute(block, "col", pair_a)
        return near_a, near_b

    packed = list(pack_rows(tentative, spans[:1]))
    packed += pack_rows(tentative, spans[1:])
    halos = [both(block) for block in packed]
    label_a, label_b = both(aggregate)
    labels = jnp.stack([label_a, aggregate, label_b])
    targets = owner_row[:, 0] * G_DEV + owner_group
    other_targets = lax.ppermute(targets, "row", flip(rows, 1))
    targets = jnp.stack([targets, other_targets])
    side = neighbour // RQ
    side = jnp.where(col % 2 == 0, 2 - side, side)
    table = jnp.where(active != 0, side * RQ + neighbour % RQ, 3 * RQ).T
    place = jnp.stack([col, row])
    labels, targets, table, place = lax.optimization_barrier((labels, targets, table, place))

    fields = []
    for (low, high), (near_a, near_b) in zip(spans, halos):
        field = prolong_rows(
            table, labels, off_blocks, diag_blocks, diag_inverse, tentative, near_a, near_b, low
        )
        fields.append((field, *both(field)))
    parts = []
    for part, ((low, high), (field, near_a, near_b)) in enumerate(zip(spans, fields)):
        keep, send = coarse_rows(
            table, place, off_blocks, diag_blocks, field, near_a, near_b, low, columns
        )
        if part == 0:
            other = lax.ppermute(send, "col", pair_a)
            total = (keep + other.astype(jnp.float32)).astype(link)
        else:
            terms = exchange(keep, send, "col", columns, 1, link)
            total = sum(term[:1].astype(jnp.float32) for term in terms).astype(link)
        other = lax.ppermute(total, "row", flip(rows, 1))
        parts.append((total, other))

    starts = [low for low, _ in spans]
    keep, *send = split_groups(targets, place, None, parts[:1], starts[:1], rows)
    terms = exchange(keep, tuple(send), "row", rows, 2, link)
    blocks = sum(term[0].astype(jnp.float32) for term in terms)
    folded = exchange(blocks[0::2], blocks[1::2].astype(link), "col", columns, 2, link)

    early = gather_groups(targets, place, parts[1:-2], starts[1:-2], rows)
    keep, *send = split_groups(targets, place, early, parts[-2:], starts[-2:], rows)
    return finish(*exchange(keep, tuple(send), "row", rows, 2, link), *folded)


def solution(mesh):
    return jax.shard_map(
        on_device,
        mesh=mesh,
        in_specs=(
            P(("row", "col"), None, None, None),
            P(("row", "col"), None),
            P(("row", "col"), None),
            P(("row", "col"), None, None),
            P(("row", "col"), None, None),
            P(("row", "col"), None, None),
            P(("row", "col")),
            P("row", None),
            P("row"),
        ),
        out_specs=P("row", "col", None),
        check_vma=False,
    )
```

profile of v0, /device:TPU:0, one launch (start us, length us, event | category | flops | bytes accessed | tf_op | source)
XLA Modules:
  0.0 148.4 jit_solution(740690206918482928)
XLA Ops:
  0.5 2.6 %collective-permute-start.1 = (s32[64]{0:T(128)}, s32[64]{0:T(128)}, u32[]{:S(2)}, u32[]{:S(2)}) collective-permute-start(s32[64]{0:T(128)} %param.15), channel_id=1, source_target_pairs={{0,3},{1,2},{2,1},{3,0},{4,7},{5,6},{6,5},{7,4},{8,11},{9,10},{10,... | collective-permute-start | bytes 776 | tf_op jit(solution)/shard_map/ppermute | solution.py:410
  3.1 1.4 copy-done.5
  4.5 1.2 shard_map.91
  6.4 2.2 %collective-permute-start.2 = (s32[32]{0:T(128)S(1)}, s32[32]{0:T(128)S(1)}, u32[]{:S(2)}, u32[]{:S(2)}) collective-permute-start(s32[32]{0:T(128)S(1)} %bitcast_add_fusion), channel_id=1, source_target_pairs={{0,4},{4,0},{8,12},{12,8},{16,20},{20,16},{24,28},{28,24},{1,5},{5... | collective-permute-start | bytes 392 | tf_op jit(solution)/shard_map/ppermute | solution.py:420
  9.2 0.9 collective-permute-done.2
  11.3 2.1 %shard_map.100 = bf16[6,96,384]{2,1,0:T(8,128)(2,1)} custom-call(bf16[64,96,96]{2,1,0:T(8,128)(2,1)} %own.7), custom_call_target="tpu_custom_call" | custom-call | bytes 1105920 | tf_op jit(solution)/shard_map/pallas_call | solution.py:55
  13.9 1.7 %collective-permute-start.28 = (bf16[6,96,384]{2,1,0:T(8,128)(2,1)}, bf16[6,96,384]{2,1,0:T(8,128)(2,1)S(1)}, u32[]{:S(2)}, u32[]{:S(2)}) collective-permute-start(bf16[6,96,384]{2,1,0:T(8,128)(2,1)} %shard_map.100), channel_id=1, source_target_pairs={{0,3},{1,2},{2,1},{3,0},{4,7},{5,6},{6,5},{7,4},{8,11},{9,10},{10,... | collective-permute-start | bytes 1327112 | tf_op jit(solution)/shard_map/ppermute | solution.py:410
  17.6 2.8 %copy-done = bf16[64,4,96,96]{3,2,1,0:T(8,128)(2,1)S(1)} copy-done((bf16[64,4,96,96]{3,2,1,0:T(8,128)(2,1)S(1)}, bf16[64,4,96,96]{3,2,1,0:T(8,128)(2,1)}, u32[]{:S(2)}) %copy-start) | copy-done | bytes 4718616
  20.4 1.4 copy-done.3
  21.8 1.4 copy-done.6
  23.2 1.4 copy-done.8
  25.3 3.2 %shard_map.95.own = bf16[8,96,384]{2,1,0:T(8,128)(2,1)S(1)} custom-call(s32[4,64]{1,0:T(4,128)S(1)} %copy-done.11, s32[3,64]{1,0:T(4,128)S(1)} %pad_add_fusion.labels, bf16[64,4,96,96]{3,2,1,0:T(8,128)(2,1)S(1)} %copy-done, bf16[64,96,96]{2,1,0:T(8,128)(2,1)S(1)} %copy-done.3, bf16[64,96,96]{2,1,0:T(8,128)(2,1)S(1)} %copy-done.8, ...), custom_call_target="tpu_custom_call" | custom-call | flops 339738624 | bytes 3244032 | tf_op jit(solution)/shard_map/pallas_call | solution.py:128
  29.4 1.8 %collective-permute-start.4 = (bf16[4,96,384]{2,1,0:T(8,128)(2,1)}, bf16[4,96,384]{2,1,0:T(8,128)(2,1)}, u32[]{:S(2)}, u32[]{:S(2)}) collective-permute-start(bf16[4,96,384]{2,1,0:T(8,128)(2,1)} %get-tuple-element.30), channel_id=1, source_target_pairs={{0,3},{1,2},{2,1},{3,0},{4,7},{5,6},{6,5},{7,4},{8,11},{9,10},{10,... | collective-permute-start | bytes 884744 | tf_op jit(solution)/shard_map/ppermute | solution.py:410
  31.3 1.7 %shard_map.97.own = bf16[4,96,384]{2,1,0:T(8,128)(2,1)S(1)} custom-call(s32[4,64]{1,0:T(4,128)S(1)} %copy-done.11, s32[3,64]{1,0:T(4,128)S(1)} %pad_add_fusion.labels, bf16[64,4,96,96]{3,2,1,0:T(8,128)(2,1)S(1)} %copy-done, bf16[64,96,96]{2,1,0:T(8,128)(2,1)S(1)} %copy-done.3, bf16[64,96,96]{2,1,0:T(8,128)(2,1)S(1)} %copy-done.8, ...), custom_call_target="tpu_custom_call" | custom-call | flops 169869312 | bytes 1622016 | tf_op jit(solution)/shard_map/pallas_call | solution.py:128
  35.0 1.0 collective-permute-start.20
  36.0 6.1 %shard_map.101.own = bf16[12,96,384]{2,1,0:T(8,128)(2,1)} custom-call(s32[4,64]{1,0:T(4,128)} %fusion.4.table, s32[3,64]{1,0:T(4,128)} %copy-done.13, bf16[64,4,96,96]{3,2,1,0:T(8,128)(2,1)} %off.15, bf16[64,96,96]{2,1,0:T(8,128)(2,1)} %diag.15, bf16[64,96,96]{2,1,0:T(8,128)(2,1)} %inverse.7, bf16[64,96,96]{2,1,0:T(8,128)(2,1)} %own.7, ...), custom_call_target="tpu_custom_call" | custom-call | flops 509607936 | bytes 4866048 | tf_op jit(solution)/shard_map/pallas_call | solution.py:128
  43.1 2.8 %copy-done.1 = bf16[64,4,96,96]{3,2,1,0:T(8,128)(2,1)S(1)} copy-done((bf16[64,4,96,96]{3,2,1,0:T(8,128)(2,1)S(1)}, bf16[64,4,96,96]{3,2,1,0:T(8,128)(2,1)}, u32[]{:S(2)}) %copy-start.1) | copy-done | bytes 4718616
  45.9 3.2 %shard_map.92.own = bf16[8,96,384]{2,1,0:T(8,128)(2,1)S(1)} custom-call(s32[4,64]{1,0:T(4,128)S(1)} %copy-done.12, s32[3,64]{1,0:T(4,128)S(1)} %copy-done.14, bf16[64,4,96,96]{3,2,1,0:T(8,128)(2,1)S(1)} %copy-done.1, bf16[64,96,96]{2,1,0:T(8,128)(2,1)S(1)} %copy-done.4, bf16[64,96,96]{2,1,0:T(8,128)(2,1)S(1)} %copy-done.9, ...), custom_call_target="tpu_custom_call" | custom-call | flops 339738624 | bytes 3244032 | tf_op jit(solution)/shard_map/pallas_call | solution.py:128
  49.2 8.7 %collective-permute-done.20.near_b = bf16[4,96,384]{2,1,0:T(8,128)(2,1)} collective-permute-done((bf16[4,96,384]{2,1,0:T(8,128)(2,1)S(1)}, bf16[4,96,384]{2,1,0:T(8,128)(2,1)}, u32[]{:S(2)}, u32[]{:S(2)}) %collective-permute-start.20) | collective-permute-done | bytes 294944 | tf_op jit(solution)/shard_map/ppermute | solution.py:410
  57.9 0.9 collective-permute-start.5
  58.7 1.4 collective-permute-start.6
  60.1 2.8 %copy-done.2 = bf16[64,4,96,96]{3,2,1,0:T(8,128)(2,1)S(1)} copy-done((bf16[64,4,96,96]{3,2,1,0:T(8,128)(2,1)S(1)}, bf16[64,4,96,96]{3,2,1,0:T(8,128)(2,1)}, u32[]{:S(2)}) %copy-start.2) | copy-done | bytes 4718616
  62.9 2.2 %shard_map.98 = (f32[2,2,48,384]{3,2,1,0:T(8,128)S(1)}, bf16[2,2,48,384]{3,2,1,0:T(8,128)(2,1)S(1)}) custom-call(s32[4,64]{1,0:T(4,128)S(1)} %copy-done.12, s32[2]{0:T(128)S(1)} %copy-done.15, bf16[64,4,96,96]{3,2,1,0:T(8,128)(2,1)S(1)} %copy-done.2, bf16[64,96,96]{2,1,0:T(8,128)(2,1)S(1)} %copy-done.4, bf16[4,96,384]{2,1,0:T(8,128)(2,1)S(1)} %shard_map.97.own, ...), custom_call_target="tpu_custom_call" | custom-call | flops 198180864 | bytes 2359296 | tf_op jit(solution)/shard_map/pallas_call | solution.py:209
  65.6 3.4 %shard_map.96 = (f32[2,4,48,384]{3,2,1,0:T(8,128)S(1)}, bf16[2,4,48,384]{3,2,1,0:T(8,128)(2,1)S(1)}) custom-call(s32[4,64]{1,0:T(4,128)S(1)} %copy-done.12, s32[2]{0:T(128)S(1)} %copy-done.15, bf16[64,4,96,96]{3,2,1,0:T(8,128)(2,1)S(1)} %copy-done.2, bf16[64,96,96]{2,1,0:T(8,128)(2,1)S(1)} %copy-done.4, bf16[8,96,384]{2,1,0:T(8,128)(2,1)S(1)} %shard_map.95.own, ...), custom_call_target="tpu_custom_call" | custom-call | flops 396361728 | bytes 4718592 | tf_op jit(solution)/shard_map/pallas_call | solution.py:209
  69.6 19.9 %collective-permute-done.6.near_b = bf16[8,96,384]{2,1,0:T(8,128)(2,1)S(1)} collective-permute-done((bf16[8,96,384]{2,1,0:T(8,128)(2,1)S(1)}, bf16[8,96,384]{2,1,0:T(8,128)(2,1)S(1)}, u32[]{:S(2)}, u32[]{:S(2)}) %collective-permute-start.6) | collective-permute-done | bytes 589856 | tf_op jit(solution)/shard_map/ppermute | solution.py:410
  89.5 2.8 %shard_map.93 = (f32[2,4,48,384]{3,2,1,0:T(8,128)S(1)}, bf16[2,4,48,384]{3,2,1,0:T(8,128)(2,1)S(1)}) custom-call(s32[4,64]{1,0:T(4,128)S(1)} %copy-done.12, s32[2]{0:T(128)S(1)} %copy-done.15, bf16[64,4,96,96]{3,2,1,0:T(8,128)(2,1)S(1)} %copy-done.2, bf16[64,96,96]{2,1,0:T(8,128)(2,1)S(1)} %copy-done.4, bf16[8,96,384]{2,1,0:T(8,128)(2,1)S(1)} %shard_map.92.own, ...), custom_call_target="tpu_custom_call" | custom-call | flops 396361728 | bytes 4718592 | tf_op jit(solution)/shard_map/pallas_call | solution.py:209
  92.9 4.0 %shard_map.102 = (f32[2,6,48,384]{3,2,1,0:T(8,128)S(1)}, bf16[2,6,48,384]{3,2,1,0:T(8,128)(2,1)S(1)}) custom-call(s32[4,64]{1,0:T(4,128)S(1)} %copy-done.12, s32[2]{0:T(128)S(1)} %copy-done.15, bf16[64,4,96,96]{3,2,1,0:T(8,128)(2,1)S(1)} %copy-done.2, bf16[64,96,96]{2,1,0:T(8,128)(2,1)S(1)} %copy-done.4, bf16[12,96,384]{2,1,0:T(8,128)(2,1)S(1)} %copy-done.10, ...), custom_call_target="tpu_custom_call" | custom-call | flops 594542592 | bytes 7077888 | tf_op jit(solution)/shard_map/pallas_call | solution.py:209
  97.1 1.9 %collective-permute-start.15 = (bf16[1,4,48,384]{3,2,1,0:T(8,128)(2,1)S(1)}, bf16[1,4,48,384]{3,2,1,0:T(8,128)(2,1)S(1)}, u32[]{:S(2)}, u32[]{:S(2)}) collective-permute-start(bf16[1,4,48,384]{3,2,1,0:T(8,128)(2,1)S(1)} %add_convert_fusion.4), channel_id=1, source_target_pairs={{0,2},{1,3},{2,0},{3,1},{4,6},{5,7},{6,4},{7,5},{8,10},{9,11},{10,... | collective-permute-start | bytes 442376 | tf_op jit(solution)/shard_map/ppermute | solution.py:375
  99.3 1.8 %collective-permute-start.32 = (bf16[2,6,48,384]{3,2,1,0:T(8,128)(2,1)S(1)}, bf16[2,6,48,384]{3,2,1,0:T(8,128)(2,1)S(1)}, u32[]{:S(2)}, u32[]{:S(2)}) collective-permute-start(bf16[2,6,48,384]{3,2,1,0:T(8,128)(2,1)S(1)} %add_convert_fusion.refs_0_), channel_id=1, source_target_pairs={{0,4},{4,0},{8,12},{12,8},{16,20},{20,16},{24,28},{28,24},{1,5},{5... | collective-permute-start | bytes 1327112 | tf_op jit(solution)/shard_map/ppermute | solution.py:445
  101.2 2.7 %collective-permute-done.15 = bf16[1,4,48,384]{3,2,1,0:T(8,128)(2,1)S(1)} collective-permute-done((bf16[1,4,48,384]{3,2,1,0:T(8,128)(2,1)S(1)}, bf16[1,4,48,384]{3,2,1,0:T(8,128)(2,1)S(1)}, u32[]{:S(2)}, u32[]{:S(2)}) %collective-permute-start.15) | collective-permute-done | bytes 147488 | tf_op jit(solution)/shard_map/ppermute | solution.py:375
  103.9 1.8 %collective-permute-start.16 = (bf16[1,4,48,384]{3,2,1,0:T(8,128)(2,1)S(1)}, bf16[1,4,48,384]{3,2,1,0:T(8,128)(2,1)S(1)}, u32[]{:S(2)}, u32[]{:S(2)}) collective-permute-start(bf16[1,4,48,384]{3,2,1,0:T(8,128)(2,1)S(1)} %add_convert_fusion.3.refs_1_), channel_id=1, source_target_pairs={{0,4},{4,0},{8,12},{12,8},{16,20},{20,16},{24,28},{28,24},{1,5},{5... | collective-permute-start | bytes 442376 | tf_op jit(solution)/shard_map/ppermute | solution.py:445
  105.7 0.8 collective-permute-done.8
  106.6 1.8 %collective-permute-start.9 = (bf16[1,4,48,384]{3,2,1,0:T(8,128)(2,1)S(1)}, bf16[1,4,48,384]{3,2,1,0:T(8,128)(2,1)S(1)}, u32[]{:S(2)}, u32[]{:S(2)}) collective-permute-start(bf16[1,4,48,384]{3,2,1,0:T(8,128)(2,1)S(1)} %add_convert_fusion.5.refs_0_), channel_id=1, source_target_pairs={{0,4},{4,0},{8,12},{12,8},{16,20},{20,16},{24,28},{28,24},{1,5},{5... | collective-permute-start | bytes 442376 | tf_op jit(solution)/shard_map/ppermute | solution.py:445
  108.4 4.1 %collective-permute-done.32.refs_1_ = bf16[2,6,48,384]{3,2,1,0:T(8,128)(2,1)S(1)} collective-permute-done((bf16[2,6,48,384]{3,2,1,0:T(8,128)(2,1)S(1)}, bf16[2,6,48,384]{3,2,1,0:T(8,128)(2,1)S(1)}, u32[]{:S(2)}, u32[]{:S(2)}) %collective-permute-start.32) | collective-permute-done | bytes 442400 | tf_op jit(solution)/shard_map/ppermute | solution.py:445
  112.5 2.2 %shard_map.103 = (f32[2,2,4,48,384]{4,3,2,1,0:T(8,128)S(1)}, bf16[1,2,4,48,384]{4,3,2,1,0:T(8,128)(2,1)S(1)}, bf16[1,2,4,48,384]{4,3,2,1,0:T(8,128)(2,1)S(1)}) custom-call(s32[2,32]{1,0:T(2,128)S(1)} %pad_add_fusion.1.targets, s32[2]{0:T(128)S(1)} %copy-done.15, bf16[2,6,48,384]{3,2,1,0:T(8,128)(2,1)S(1)} %add_convert_fusion.refs_0_, ...), custom_call_target="tpu_custom_call" | custom-call | flops 589824 | bytes 14745600 | tf_op jit(solution)/shard_map/pallas_call | solution.py:327
  114.7 1.9 %collective-permute-start.34 = (bf16[1,2,4,48,384]{4,3,2,1,0:T(8,128)(2,1)S(1)}, bf16[1,2,4,48,384]{4,3,2,1,0:T(8,128)(2,1)S(1)}, u32[]{:S(2)}, u32[]{:S(2)}) collective-permute-start(bf16[1,2,4,48,384]{4,3,2,1,0:T(8,128)(2,1)S(1)} %get-tuple-element.46), channel_id=1, source_target_pairs={{0,8},{4,12},{8,0},{12,4},{16,24},{20,28},{24,16},{28,20},{1,9},{5... | collective-permute-start | bytes 884744 | tf_op jit(solution)/shard_map/ppermute | solution.py:372
  116.7 1.6 %collective-permute-start.23 = (bf16[1,2,48,384]{3,2,1,0:T(8,128)(2,1)S(1)}, bf16[1,2,48,384]{3,2,1,0:T(8,128)(2,1)S(1)}, u32[]{:S(2)}, u32[]{:S(2)}) collective-permute-start(bf16[1,2,48,384]{3,2,1,0:T(8,128)(2,1)S(1)} %add_convert_fusion.7.refs_3_), channel_id=1, source_target_pairs={{0,4},{4,0},{8,12},{12,8},{16,20},{20,16},{24,28},{28,24},{1,5},{5... | collective-permute-start | bytes 221192 | tf_op jit(solution)/shard_map/ppermute | solution.py:445
  118.5 1.3 shard_map.94.refs_0_
  119.8 1.3 collective-permute-done.23.refs_4_
  121.1 1.9 %shard_map.99 = (f32[2,1,4,48,384]{4,3,2,1,0:T(8,128)S(1)}, bf16[1,1,4,48,384]{4,3,2,1,0:T(8,128)(2,1)S(1)}, bf16[1,1,4,48,384]{4,3,2,1,0:T(8,128)(2,1)S(1)}) custom-call(s32[2,32]{1,0:T(2,128)S(1)} %pad_add_fusion.1.targets, s32[2]{0:T(128)S(1)} %copy-done.15, f32[33,48,192]{2,1,0:T(8,128)S(1)} %shard_map.94.refs_0_, ...), custom_call_target="tpu_custom_call" | custom-call | flops 589824 | bytes 14745600 | tf_op jit(solution)/shard_map/pallas_call | solution.py:327
  123.6 1.5 %collective-permute-start.33 = (bf16[1,2,4,48,384]{4,3,2,1,0:T(8,128)(2,1)S(1)}, bf16[1,2,4,48,384]{4,3,2,1,0:T(8,128)(2,1)S(1)}, u32[]{:S(2)}, u32[]{:S(2)}) collective-permute-start(bf16[1,2,4,48,384]{4,3,2,1,0:T(8,128)(2,1)S(1)} %get-tuple-element.45), channel_id=1, source_target_pairs={{0,8},{4,12},{8,0},{12,4},{16,24},{20,28},{24,16},{28,20},{1,9},{5... | collective-permute-start | bytes 884744 | tf_op jit(solution)/shard_map/ppermute | solution.py:373
  125.1 2.6 %collective-permute-start.35 = (bf16[1,2,4,48,384]{4,3,2,1,0:T(8,128)(2,1)S(1)}, bf16[1,2,4,48,384]{4,3,2,1,0:T(8,128)(2,1)S(1)}, u32[]{:S(2)}, u32[]{:S(2)}) collective-permute-start(bf16[1,2,4,48,384]{4,3,2,1,0:T(8,128)(2,1)S(1)} %add_convert_fusion.1), channel_id=1, source_target_pairs={{0,16},{4,20},{8,24},{12,28},{16,0},{20,4},{24,8},{28,12},{1,17},{... | collective-permute-start | bytes 884744 | tf_op jit(solution)/shard_map/ppermute | solution.py:375
  128.3 8.5 %collective-permute-done.25 = bf16[1,1,4,48,384]{4,3,2,1,0:T(8,128)(2,1)S(1)} collective-permute-done((bf16[1,1,4,48,384]{4,3,2,1,0:T(8,128)(2,1)S(1)}, bf16[1,1,4,48,384]{4,3,2,1,0:T(8,128)(2,1)S(1)}, u32[]{:S(2)}, u32[]{:S(2)}) %collective-permute-start.25) | collective-permute-done | bytes 147488 | tf_op jit(solution)/shard_map/ppermute | solution.py:372
  137.1 5.1 %collective-permute-done.33 = bf16[1,2,4,48,384]{4,3,2,1,0:T(8,128)(2,1)S(1)} collective-permute-done((bf16[1,2,4,48,384]{4,3,2,1,0:T(8,128)(2,1)S(1)}, bf16[1,2,4,48,384]{4,3,2,1,0:T(8,128)(2,1)S(1)}, u32[]{:S(2)}, u32[]{:S(2)}) %collective-permute-start.33) | collective-permute-done | bytes 294944 | tf_op jit(solution)/shard_map/ppermute | solution.py:373
  142.3 1.6 %collective-permute-start.36 = (bf16[1,4,48,384]{3,2,1,0:T(8,128)(2,1)S(1)}, bf16[1,4,48,384]{3,2,1,0:T(8,128)(2,1)S(1)}, u32[]{:S(2)}, u32[]{:S(2)}) collective-permute-start(bf16[1,4,48,384]{3,2,1,0:T(8,128)(2,1)S(1)} %fusion), channel_id=1, source_target_pairs={{0,2},{1,3},{2,0},{3,1},{4,6},{5,7},{6,4},{7,5},{8,10},{9,11},{10,... | collective-permute-start | bytes 442376 | tf_op jit(solution)/shard_map/ppermute | solution.py:375
  143.9 1.8 %collective-permute-done.26.refs_2_ = bf16[1,1,4,48,384]{4,3,2,1,0:T(8,128)(2,1)S(1)} collective-permute-done((bf16[1,1,4,48,384]{4,3,2,1,0:T(8,128)(2,1)S(1)}, bf16[1,1,4,48,384]{4,3,2,1,0:T(8,128)(2,1)S(1)}, u32[]{:S(2)}, u32[]{:S(2)}) %collective-permute-start.26) | collective-permute-done | bytes 147488 | tf_op jit(solution)/shard_map/ppermute | solution.py:375
  145.7 1.8 %collective-permute-done.36.refs_4_ = bf16[1,4,48,384]{3,2,1,0:T(8,128)(2,1)S(1)} collective-permute-done((bf16[1,4,48,384]{3,2,1,0:T(8,128)(2,1)S(1)}, bf16[1,4,48,384]{3,2,1,0:T(8,128)(2,1)S(1)}, u32[]{:S(2)}, u32[]{:S(2)}) %collective-permute-start.36) | collective-permute-done | bytes 147488 | tf_op jit(solution)/shard_map/ppermute | solution.py:375
  147.5 0.9 shard_map.104
  (107 shorter events, 14.3 us)
Async XLA Ops:
  0.0 13.4 %collective-permute-start = (s32[64]{0:T(128)}, s32[64]{0:T(128)}, u32[]{:S(2)}, u32[]{:S(2)}) collective-permute-start(s32[64]{0:T(128)} %param.15), channel_id=1, source_target_pairs={{0,1},{1,0},{2,3},{3,2},{4,5},{5,4},{6,7},{7,6},{8,9},{9,8},{10,11... | collective-permute-start | bytes 776 | tf_op jit(solution)/shard_map/ppermute | solution.py:411
  0.5 13.4 %collective-permute-start.1 = (s32[64]{0:T(128)}, s32[64]{0:T(128)}, u32[]{:S(2)}, u32[]{:S(2)}) collective-permute-start(s32[64]{0:T(128)} %param.15), channel_id=1, source_target_pairs={{0,3},{1,2},{2,1},{3,0},{4,7},{5,6},{6,5},{7,4},{8,11},{9,10},{10,... | collective-permute-start | bytes 776 | tf_op jit(solution)/shard_map/ppermute | solution.py:410
  4.5 4.0 %copy-start.19 = (s32[64,4]{0,1:T(4,128)S(1)}, s32[64,4]{0,1:T(4,128)}, u32[]{:S(2)}) copy-start(s32[64,4]{0,1:T(4,128)} %param.10) | copy-start | bytes 3076
  4.5 4.0 %copy-start.20 = (s32[64,4]{0,1:T(4,128)S(1)}, s32[64,4]{0,1:T(4,128)}, u32[]{:S(2)}) copy-start(s32[64,4]{0,1:T(4,128)} %param.11) | copy-start | bytes 3076
  6.4 9.3 %collective-permute-start.10 = (bf16[4,96,384]{2,1,0:T(8,128)(2,1)}, bf16[4,96,384]{2,1,0:T(8,128)(2,1)}, u32[]{:S(2)}, u32[]{:S(2)}) collective-permute-start(bf16[4,96,384]{2,1,0:T(8,128)(2,1)} %get-tuple-element.33), channel_id=1, source_target_pairs={{0,1},{1,0},{2,3},{3,2},{4,5},{5,4},{6,7},{7,6},{8,9},{9,8},{10,11... | collective-permute-start | bytes 884744 | tf_op jit(solution)/shard_map/ppermute | solution.py:411
  6.4 10.4 %collective-permute-start.11 = (bf16[4,96,384]{2,1,0:T(8,128)(2,1)}, bf16[4,96,384]{2,1,0:T(8,128)(2,1)}, u32[]{:S(2)}, u32[]{:S(2)}) collective-permute-start(bf16[4,96,384]{2,1,0:T(8,128)(2,1)} %get-tuple-element.33), channel_id=1, source_target_pairs={{0,3},{1,2},{2,1},{3,0},{4,7},{5,6},{6,5},{7,4},{8,11},{9,10},{10,... | collective-permute-start | bytes 884744 | tf_op jit(solution)/shard_map/ppermute | solution.py:410
  6.4 3.7 %collective-permute-start.2 = (s32[32]{0:T(128)S(1)}, s32[32]{0:T(128)S(1)}, u32[]{:S(2)}, u32[]{:S(2)}) collective-permute-start(s32[32]{0:T(128)S(1)} %bitcast_add_fusion), channel_id=1, source_target_pairs={{0,4},{4,0},{8,12},{12,8},{16,20},{20,16},{24,28},{28,24},{1,5},{5... | collective-permute-start | bytes 392 | tf_op jit(solution)/shard_map/ppermute | solution.py:420
  10.7 22.3 %collective-permute-start.3 = (bf16[4,96,384]{2,1,0:T(8,128)(2,1)}, bf16[4,96,384]{2,1,0:T(8,128)(2,1)}, u32[]{:S(2)}, u32[]{:S(2)}) collective-permute-start(bf16[4,96,384]{2,1,0:T(8,128)(2,1)} %get-tuple-element.30), channel_id=1, source_target_pairs={{0,1},{1,0},{2,3},{3,2},{4,5},{5,4},{6,7},{7,6},{8,9},{9,8},{10,11... | collective-permute-start | bytes 884744 | tf_op jit(solution)/shard_map/ppermute | solution.py:411
  13.4 20.1 %collective-permute-start.27 = (bf16[6,96,384]{2,1,0:T(8,128)(2,1)}, bf16[6,96,384]{2,1,0:T(8,128)(2,1)S(1)}, u32[]{:S(2)}, u32[]{:S(2)}) collective-permute-start(bf16[6,96,384]{2,1,0:T(8,128)(2,1)} %shard_map.100), channel_id=1, source_target_pairs={{0,1},{1,0},{2,3},{3,2},{4,5},{5,4},{6,7},{7,6},{8,9},{9,8},{10,11... | collective-permute-start | bytes 1327112 | tf_op jit(solution)/shard_map/ppermute | solution.py:411
  13.9 19.6 %collective-permute-start.28 = (bf16[6,96,384]{2,1,0:T(8,128)(2,1)}, bf16[6,96,384]{2,1,0:T(8,128)(2,1)S(1)}, u32[]{:S(2)}, u32[]{:S(2)}) collective-permute-start(bf16[6,96,384]{2,1,0:T(8,128)(2,1)} %shard_map.100), channel_id=1, source_target_pairs={{0,3},{1,2},{2,1},{3,0},{4,7},{5,6},{6,5},{7,4},{8,11},{9,10},{10,... | collective-permute-start | bytes 1327112 | tf_op jit(solution)/shard_map/ppermute | solution.py:410
  15.7 12.9 %collective-permute-start.17 = (bf16[2,96,384]{2,1,0:T(8,128)(2,1)}, bf16[2,96,384]{2,1,0:T(8,128)(2,1)S(1)}, u32[]{:S(2)}, u32[]{:S(2)}) collective-permute-start(bf16[2,96,384]{2,1,0:T(8,128)(2,1)} %copy-done.16), channel_id=1, source_target_pairs={{0,1},{1,0},{2,3},{3,2},{4,5},{5,4},{6,7},{7,6},{8,9},{9,8},{10,11... | collective-permute-start | bytes 442376 | tf_op jit(solution)/shard_map/ppermute | solution.py:411
  16.8 12.7 %collective-permute-start.18 = (bf16[2,96,384]{2,1,0:T(8,128)(2,1)}, bf16[2,96,384]{2,1,0:T(8,128)(2,1)S(1)}, u32[]{:S(2)}, u32[]{:S(2)}) collective-permute-start(bf16[2,96,384]{2,1,0:T(8,128)(2,1)} %copy-done.16), channel_id=1, source_target_pairs={{0,3},{1,2},{2,1},{3,0},{4,7},{5,6},{6,5},{7,4},{8,11},{9,10},{10,... | collective-permute-start | bytes 442376 | tf_op jit(solution)/shard_map/ppermute | solution.py:410
  25.3 6.0 %copy-start.13 = (s32[3,64]{1,0:T(4,128)}, s32[3,64]{1,0:T(4,128)S(1)}, u32[]{:S(2)}) copy-start(s32[3,64]{1,0:T(4,128)S(1)} %pad_add_fusion.labels) | copy-start | bytes 2308
  28.6 30.2 %collective-permute-start.12 = (bf16[8,96,384]{2,1,0:T(8,128)(2,1)S(1)}, bf16[8,96,384]{2,1,0:T(8,128)(2,1)S(1)}, u32[]{:S(2)}, u32[]{:S(2)}) collective-permute-start(bf16[8,96,384]{2,1,0:T(8,128)(2,1)S(1)} %shard_map.95.own), channel_id=1, source_target_pairs={{0,1},{1,0},{2,3},{3,2},{4,5},{5,4},{6,7},{7,6},{8,9},{9,8},{10,11... | collective-permute-start | bytes 1769480 | tf_op jit(solution)/shard_map/ppermute | solution.py:411
  29.4 12.7 %collective-permute-start.4 = (bf16[4,96,384]{2,1,0:T(8,128)(2,1)}, bf16[4,96,384]{2,1,0:T(8,128)(2,1)}, u32[]{:S(2)}, u32[]{:S(2)}) collective-permute-start(bf16[4,96,384]{2,1,0:T(8,128)(2,1)} %get-tuple-element.30), channel_id=1, source_target_pairs={{0,3},{1,2},{2,1},{3,0},{4,7},{5,6},{6,5},{7,4},{8,11},{9,10},{10,... | collective-permute-start | bytes 884744 | tf_op jit(solution)/shard_map/ppermute | solution.py:410
  33.0 10.1 %copy-start.4 = (bf16[64,96,96]{2,1,0:T(8,128)(2,1)S(1)}, bf16[64,96,96]{2,1,0:T(8,128)(2,1)}, u32[]{:S(2)}) copy-start(bf16[64,96,96]{2,1,0:T(8,128)(2,1)} %diag.15) | copy-start | bytes 3538948
  33.0 10.1 %copy-start.7 = (bf16[64,96,96]{2,1,0:T(8,128)(2,1)S(1)}, bf16[64,96,96]{2,1,0:T(8,128)(2,1)}, u32[]{:S(2)}) copy-start(bf16[64,96,96]{2,1,0:T(8,128)(2,1)} %own.7) | copy-start | bytes 3538948
  33.0 10.1 %copy-start.9 = (bf16[64,96,96]{2,1,0:T(8,128)(2,1)S(1)}, bf16[64,96,96]{2,1,0:T(8,128)(2,1)}, u32[]{:S(2)}) copy-start(bf16[64,96,96]{2,1,0:T(8,128)(2,1)} %inverse.7) | copy-start | bytes 3538948
  33.0 10.1 %copy-start.12 = (s32[4,64]{1,0:T(4,128)S(1)}, s32[4,64]{1,0:T(4,128)}, u32[]{:S(2)}) copy-start(s32[4,64]{1,0:T(4,128)} %fusion.4.table) | copy-start | bytes 3076
  33.0 10.1 %copy-start.14 = (s32[3,64]{1,0:T(4,128)S(1)}, s32[3,64]{1,0:T(4,128)}, u32[]{:S(2)}) copy-start(s32[3,64]{1,0:T(4,128)} %copy-done.13) | copy-start | bytes 2308
  33.0 9.3 %collective-permute-start.19 = (bf16[4,96,384]{2,1,0:T(8,128)(2,1)S(1)}, bf16[4,96,384]{2,1,0:T(8,128)(2,1)}, u32[]{:S(2)}, u32[]{:S(2)}) collective-permute-start(bf16[4,96,384]{2,1,0:T(8,128)(2,1)S(1)} %shard_map.97.own), channel_id=1, source_target_pairs={{0,1},{1,0},{2,3},{3,2},{4,5},{5,4},{6,7},{7,6},{8,9},{9,8},{10,11... | collective-permute-start | bytes 884744 | tf_op jit(solution)/shard_map/ppermute | solution.py:411
  33.5 31.5 %collective-permute-start.13 = (bf16[8,96,384]{2,1,0:T(8,128)(2,1)S(1)}, bf16[8,96,384]{2,1,0:T(8,128)(2,1)}, u32[]{:S(2)}, u32[]{:S(2)}) collective-permute-start(bf16[8,96,384]{2,1,0:T(8,128)(2,1)S(1)} %shard_map.95.own), channel_id=1, source_target_pairs={{0,3},{1,2},{2,1},{3,0},{4,7},{5,6},{6,5},{7,4},{8,11},{9,10},{10,... | collective-permute-start | bytes 1769480 | tf_op jit(solution)/shard_map/ppermute | solution.py:410
  35.0 22.8 %collective-permute-start.20 = (bf16[4,96,384]{2,1,0:T(8,128)(2,1)S(1)}, bf16[4,96,384]{2,1,0:T(8,128)(2,1)}, u32[]{:S(2)}, u32[]{:S(2)}) collective-permute-start(bf16[4,96,384]{2,1,0:T(8,128)(2,1)S(1)} %shard_map.97.own), channel_id=1, source_target_pairs={{0,3},{1,2},{2,1},{3,0},{4,7},{5,6},{6,5},{7,4},{8,11},{9,10},{10,... | collective-permute-start | bytes 884744 | tf_op jit(solution)/shard_map/ppermute | solution.py:410
  36.0 24.1 %copy-start.15 = (s32[2]{0:T(128)S(1)}, s32[2]{0:T(128)}, u32[]{:S(2)}) copy-start(s32[2]{0:T(128)} %pad_add_fusion.2.place) | copy-start | bytes 28
  42.1 50.8 %collective-permute-start.29 = (bf16[12,96,384]{2,1,0:T(8,128)(2,1)}, bf16[12,96,384]{2,1,0:T(8,128)(2,1)S(1)}, u32[]{:S(2)}, u32[]{:S(2)}) collective-permute-start(bf16[12,96,384]{2,1,0:T(8,128)(2,1)} %shard_map.101.own), channel_id=1, source_target_pairs={{0,1},{1,0},{2,3},{3,2},{4,5},{5,4},{6,7},{7,6},{8,9},{9,8},{10,11... | collective-permute-start | bytes 2654216 | tf_op jit(solution)/shard_map/ppermute | solution.py:411
  42.3 50.6 %collective-permute-start.30 = (bf16[12,96,384]{2,1,0:T(8,128)(2,1)}, bf16[12,96,384]{2,1,0:T(8,128)(2,1)S(1)}, u32[]{:S(2)}, u32[]{:S(2)}) collective-permute-start(bf16[12,96,384]{2,1,0:T(8,128)(2,1)} %shard_map.101.own), channel_id=1, source_target_pairs={{0,3},{1,2},{2,1},{3,0},{4,7},{5,6},{6,5},{7,4},{8,11},{9,10},{10,... | collective-permute-start | bytes 2654216 | tf_op jit(solution)/shard_map/ppermute | solution.py:410
  43.1 2.8 %copy-start.1 = (bf16[64,4,96,96]{3,2,1,0:T(8,128)(2,1)S(1)}, bf16[64,4,96,96]{3,2,1,0:T(8,128)(2,1)}, u32[]{:S(2)}) copy-start(bf16[64,4,96,96]{3,2,1,0:T(8,128)(2,1)} %off.15) | copy-start | bytes 14155780
  57.9 11.3 %collective-permute-start.5 = (bf16[8,96,384]{2,1,0:T(8,128)(2,1)S(1)}, bf16[8,96,384]{2,1,0:T(8,128)(2,1)S(1)}, u32[]{:S(2)}, u32[]{:S(2)}) collective-permute-start(bf16[8,96,384]{2,1,0:T(8,128)(2,1)S(1)} %shard_map.92.own), channel_id=1, source_target_pairs={{0,1},{1,0},{2,3},{3,2},{4,5},{5,4},{6,7},{7,6},{8,9},{9,8},{10,11... | collective-permute-start | bytes 1769480 | tf_op jit(solution)/shard_map/ppermute | solution.py:411
  58.7 30.7 %collective-permute-start.6 = (bf16[8,96,384]{2,1,0:T(8,128)(2,1)S(1)}, bf16[8,96,384]{2,1,0:T(8,128)(2,1)S(1)}, u32[]{:S(2)}, u32[]{:S(2)}) collective-permute-start(bf16[8,96,384]{2,1,0:T(8,128)(2,1)S(1)} %shard_map.92.own), channel_id=1, source_target_pairs={{0,3},{1,2},{2,1},{3,0},{4,7},{5,6},{6,5},{7,4},{8,11},{9,10},{10,... | collective-permute-start | bytes 1769480 | tf_op jit(solution)/shard_map/ppermute | solution.py:410
  65.0 3.9 %collective-permute-start.21 = (bf16[2,2,48,384]{3,2,1,0:T(8,128)(2,1)S(1)}, bf16[2,2,48,384]{3,2,1,0:T(8,128)(2,1)S(1)}, u32[]{:S(2)}, u32[]{:S(2)}) collective-permute-start(bf16[2,2,48,384]{3,2,1,0:T(8,128)(2,1)S(1)} %get-tuple-element.38), channel_id=1, source_target_pairs={{0,1},{1,0},{2,3},{3,2},{4,5},{5,4},{6,7},{7,6},{8,9},{9,8},{10,11... | collective-permute-start | bytes 442376 | tf_op jit(solution)/shard_map/ppermute | solution.py:375
  69.0 28.0 %collective-permute-start.14 = (bf16[2,4,48,384]{3,2,1,0:T(8,128)(2,1)S(1)}, bf16[2,4,48,384]{3,2,1,0:T(8,128)(2,1)S(1)}, u32[]{:S(2)}, u32[]{:S(2)}) collective-permute-start(bf16[2,4,48,384]{3,2,1,0:T(8,128)(2,1)S(1)} %get-tuple-element.35), channel_id=1, source_target_pairs={{0,1},{1,0},{2,3},{3,2},{4,5},{5,4},{6,7},{7,6},{8,9},{9,8},{10,11... | collective-permute-start | bytes 884744 | tf_op jit(solution)/shard_map/ppermute | solution.py:375
  69.1 23.8 %copy-start.10 = (bf16[12,96,384]{2,1,0:T(8,128)(2,1)S(1)}, bf16[12,96,384]{2,1,0:T(8,128)(2,1)}, u32[]{:S(2)}) copy-start(bf16[12,96,384]{2,1,0:T(8,128)(2,1)} %shard_map.101.own) | copy-start | bytes 2654212
  69.1 47.5 %collective-permute-start.22 = (bf16[1,2,48,384]{3,2,1,0:T(8,128)(2,1)S(1)}, bf16[1,2,48,384]{3,2,1,0:T(8,128)(2,1)S(1)}, u32[]{:S(2)}, u32[]{:S(2)}) collective-permute-start(bf16[1,2,48,384]{3,2,1,0:T(8,128)(2,1)S(1)} %add_convert_fusion.8), channel_id=1, source_target_pairs={{0,2},{1,3},{2,0},{3,1},{4,6},{5,7},{6,4},{7,5},{8,10},{9,11},{10,... | collective-permute-start | bytes 221192 | tf_op jit(solution)/shard_map/ppermute | solution.py:375
  92.3 6.6 %collective-permute-start.7 = (bf16[2,4,48,384]{3,2,1,0:T(8,128)(2,1)S(1)}, bf16[2,4,48,384]{3,2,1,0:T(8,128)(2,1)S(1)}, u32[]{:S(2)}, u32[]{:S(2)}) collective-permute-start(bf16[2,4,48,384]{3,2,1,0:T(8,128)(2,1)S(1)} %get-tuple-element.32), channel_id=1, source_target_pairs={{0,1},{1,0},{2,3},{3,2},{4,5},{5,4},{6,7},{7,6},{8,9},{9,8},{10,11... | collective-permute-start | bytes 884744 | tf_op jit(solution)/shard_map/ppermute | solution.py:375
  96.9 2.3 %collective-permute-start.31 = (bf16[2,6,48,384]{3,2,1,0:T(8,128)(2,1)S(1)}, bf16[2,6,48,384]{3,2,1,0:T(8,128)(2,1)S(1)}, u32[]{:S(2)}, u32[]{:S(2)}) collective-permute-start(bf16[2,6,48,384]{3,2,1,0:T(8,128)(2,1)S(1)} %get-tuple-element.43), channel_id=1, source_target_pairs={{0,1},{1,0},{2,3},{3,2},{4,5},{5,4},{6,7},{7,6},{8,9},{9,8},{10,11... | collective-permute-start | bytes 1327112 | tf_op jit(solution)/shard_map/ppermute | solution.py:440
  97.1 6.8 %collective-permute-start.15 = (bf16[1,4,48,384]{3,2,1,0:T(8,128)(2,1)S(1)}, bf16[1,4,48,384]{3,2,1,0:T(8,128)(2,1)S(1)}, u32[]{:S(2)}, u32[]{:S(2)}) collective-permute-start(bf16[1,4,48,384]{3,2,1,0:T(8,128)(2,1)S(1)} %add_convert_fusion.4), channel_id=1, source_target_pairs={{0,2},{1,3},{2,0},{3,1},{4,6},{5,7},{6,4},{7,5},{8,10},{9,11},{10,... | collective-permute-start | bytes 442376 | tf_op jit(solution)/shard_map/ppermute | solution.py:375
  99.0 7.5 %collective-permute-start.8 = (bf16[1,4,48,384]{3,2,1,0:T(8,128)(2,1)S(1)}, bf16[1,4,48,384]{3,2,1,0:T(8,128)(2,1)S(1)}, u32[]{:S(2)}, u32[]{:S(2)}) collective-permute-start(bf16[1,4,48,384]{3,2,1,0:T(8,128)(2,1)S(1)} %add_convert_fusion.6), channel_id=1, source_target_pairs={{0,2},{1,3},{2,0},{3,1},{4,6},{5,7},{6,4},{7,5},{8,10},{9,11},{10,... | collective-permute-start | bytes 442376 | tf_op jit(solution)/shard_map/ppermute | solution.py:375
  99.3 13.1 %collective-permute-start.32 = (bf16[2,6,48,384]{3,2,1,0:T(8,128)(2,1)S(1)}, bf16[2,6,48,384]{3,2,1,0:T(8,128)(2,1)S(1)}, u32[]{:S(2)}, u32[]{:S(2)}) collective-permute-start(bf16[2,6,48,384]{3,2,1,0:T(8,128)(2,1)S(1)} %add_convert_fusion.refs_0_), channel_id=1, source_target_pairs={{0,4},{4,0},{8,12},{12,8},{16,20},{20,16},{24,28},{28,24},{1,5},{5... | collective-permute-start | bytes 1327112 | tf_op jit(solution)/shard_map/ppermute | solution.py:445
  103.9 17.2 %collective-permute-start.16 = (bf16[1,4,48,384]{3,2,1,0:T(8,128)(2,1)S(1)}, bf16[1,4,48,384]{3,2,1,0:T(8,128)(2,1)S(1)}, u32[]{:S(2)}, u32[]{:S(2)}) collective-permute-start(bf16[1,4,48,384]{3,2,1,0:T(8,128)(2,1)S(1)} %add_convert_fusion.3.refs_1_), channel_id=1, source_target_pairs={{0,4},{4,0},{8,12},{12,8},{16,20},{20,16},{24,28},{28,24},{1,5},{5... | collective-permute-start | bytes 442376 | tf_op jit(solution)/shard_map/ppermute | solution.py:445
  106.6 12.0 %collective-permute-start.9 = (bf16[1,4,48,384]{3,2,1,0:T(8,128)(2,1)S(1)}, bf16[1,4,48,384]{3,2,1,0:T(8,128)(2,1)S(1)}, u32[]{:S(2)}, u32[]{:S(2)}) collective-permute-start(bf16[1,4,48,384]{3,2,1,0:T(8,128)(2,1)S(1)} %add_convert_fusion.5.refs_0_), channel_id=1, source_target_pairs={{0,4},{4,0},{8,12},{12,8},{16,20},{20,16},{24,28},{28,24},{1,5},{5... | collective-permute-start | bytes 442376 | tf_op jit(solution)/shard_map/ppermute | solution.py:445
  114.7 10.4 %collective-permute-start.34 = (bf16[1,2,4,48,384]{4,3,2,1,0:T(8,128)(2,1)S(1)}, bf16[1,2,4,48,384]{4,3,2,1,0:T(8,128)(2,1)S(1)}, u32[]{:S(2)}, u32[]{:S(2)}) collective-permute-start(bf16[1,2,4,48,384]{4,3,2,1,0:T(8,128)(2,1)S(1)} %get-tuple-element.46), channel_id=1, source_target_pairs={{0,8},{4,12},{8,0},{12,4},{16,24},{20,28},{24,16},{28,20},{1,9},{5... | collective-permute-start | bytes 884744 | tf_op jit(solution)/shard_map/ppermute | solution.py:372
  116.7 4.4 %collective-permute-start.23 = (bf16[1,2,48,384]{3,2,1,0:T(8,128)(2,1)S(1)}, bf16[1,2,48,384]{3,2,1,0:T(8,128)(2,1)S(1)}, u32[]{:S(2)}, u32[]{:S(2)}) collective-permute-start(bf16[1,2,48,384]{3,2,1,0:T(8,128)(2,1)S(1)} %add_convert_fusion.7.refs_3_), channel_id=1, source_target_pairs={{0,4},{4,0},{8,12},{12,8},{16,20},{20,16},{24,28},{28,24},{1,5},{5... | collective-permute-start | bytes 221192 | tf_op jit(solution)/shard_map/ppermute | solution.py:445
  123.0 13.8 %collective-permute-start.25 = (bf16[1,1,4,48,384]{4,3,2,1,0:T(8,128)(2,1)S(1)}, bf16[1,1,4,48,384]{4,3,2,1,0:T(8,128)(2,1)S(1)}, u32[]{:S(2)}, u32[]{:S(2)}) collective-permute-start(bf16[1,1,4,48,384]{4,3,2,1,0:T(8,128)(2,1)S(1)} %get-tuple-element.41), channel_id=1, source_target_pairs={{0,8},{4,12},{8,0},{12,4},{16,24},{20,28},{24,16},{28,20},{1,9},{5... | collective-permute-start | bytes 442376 | tf_op jit(solution)/shard_map/ppermute | solution.py:372
  123.6 18.6 %collective-permute-start.33 = (bf16[1,2,4,48,384]{4,3,2,1,0:T(8,128)(2,1)S(1)}, bf16[1,2,4,48,384]{4,3,2,1,0:T(8,128)(2,1)S(1)}, u32[]{:S(2)}, u32[]{:S(2)}) collective-permute-start(bf16[1,2,4,48,384]{4,3,2,1,0:T(8,128)(2,1)S(1)} %get-tuple-element.45), channel_id=1, source_target_pairs={{0,8},{4,12},{8,0},{12,4},{16,24},{20,28},{24,16},{28,20},{1,9},{5... | collective-permute-start | bytes 884744 | tf_op jit(solution)/shard_map/ppermute | solution.py:373
  125.1 17.0 %collective-permute-start.35 = (bf16[1,2,4,48,384]{4,3,2,1,0:T(8,128)(2,1)S(1)}, bf16[1,2,4,48,384]{4,3,2,1,0:T(8,128)(2,1)S(1)}, u32[]{:S(2)}, u32[]{:S(2)}) collective-permute-start(bf16[1,2,4,48,384]{4,3,2,1,0:T(8,128)(2,1)S(1)} %add_convert_fusion.1), channel_id=1, source_target_pairs={{0,16},{4,20},{8,24},{12,28},{16,0},{20,4},{24,8},{28,12},{1,17},{... | collective-permute-start | bytes 884744 | tf_op jit(solution)/shard_map/ppermute | solution.py:375
  127.8 16.1 %collective-permute-start.24 = (bf16[1,1,4,48,384]{4,3,2,1,0:T(8,128)(2,1)S(1)}, bf16[1,1,4,48,384]{4,3,2,1,0:T(8,128)(2,1)S(1)}, u32[]{:S(2)}, u32[]{:S(2)}) collective-permute-start(bf16[1,1,4,48,384]{4,3,2,1,0:T(8,128)(2,1)S(1)} %get-tuple-element.40), channel_id=1, source_target_pairs={{0,8},{4,12},{8,0},{12,4},{16,24},{20,28},{24,16},{28,20},{1,9},{5... | collective-permute-start | bytes 442376 | tf_op jit(solution)/shard_map/ppermute | solution.py:373
  136.8 8.9 %collective-permute-start.26 = (bf16[1,1,4,48,384]{4,3,2,1,0:T(8,128)(2,1)S(1)}, bf16[1,1,4,48,384]{4,3,2,1,0:T(8,128)(2,1)S(1)}, u32[]{:S(2)}, u32[]{:S(2)}) collective-permute-start(bf16[1,1,4,48,384]{4,3,2,1,0:T(8,128)(2,1)S(1)} %add_convert_fusion.2), channel_id=1, source_target_pairs={{0,16},{4,20},{8,24},{12,28},{16,0},{20,4},{24,8},{28,12},{1,17},{... | collective-permute-start | bytes 442376 | tf_op jit(solution)/shard_map/ppermute | solution.py:375
  142.3 5.2 %collective-permute-start.36 = (bf16[1,4,48,384]{3,2,1,0:T(8,128)(2,1)S(1)}, bf16[1,4,48,384]{3,2,1,0:T(8,128)(2,1)S(1)}, u32[]{:S(2)}, u32[]{:S(2)}) collective-permute-start(bf16[1,4,48,384]{3,2,1,0:T(8,128)(2,1)S(1)} %fusion), channel_id=1, source_target_pairs={{0,2},{1,3},{2,0},{3,1},{4,6},{5,7},{6,4},{7,5},{8,10},{9,11},{10,... | collective-permute-start | bytes 442376 | tf_op jit(solution)/shard_map/ppermute | solution.py:375
  (14 other events, 21.1 us)
where the time goes:
time: 149 us; the launch traced here: 148 us
  waiting for transfers between devices  56.6 us (38%)
  Pallas kernels  36.2 us (24%)
  starting transfers between devices  34.7 us (23%)
  local copies, waits for them, and re-layouts  17.5 us (12%)
  other arithmetic  3.01 us (2%)
    ppermute x9, waiting for transfers between devices, both(): near_b = lax.ppermute(block, 'col', pair_b)  29.3 us
    unnamed x50, local copies, waits for them, and re-layouts  17.5 us
    pallas_call x4, Pallas kernels, prolong_rows(): pl.pallas_call(functools.partial(prolong_kernel, first), grid=(count // s...  14.3 us
    pallas_call x4, Pallas kernels, coarse_rows(): pl.pallas_call(functools.partial(coarse_kernel, first), grid=(count // st...  12.3 us
    ppermute x9, starting transfers between devices, both(): near_b = lax.ppermute(block, 'col', pair_b)  9.43 us
    ppermute x2, waiting for transfers between devices, exchange(): odd = lax.ppermute(send[0], axis, route)  8.5 us
    ppermute x9, starting transfers between devices, exchange(): arrived = (lax.ppermute(send, axis, route), 2)  8.39 us
    ppermute x9, waiting for transfers between devices, exchange(): arrived = (lax.ppermute(send, axis, route), 2)  7.04 us
  transfers between devices with their start and end apart: 37, of which 13 were waited for; matrix products, arithmetic and copies ran while one was open for 2% of the time, Pallas kernels for 24%

commit v1 on v0

--- a/solution.py
+++ b/solution.py
@@ -13,7 +13,8 @@
 G_DEV = 8
 OMEGA = 0.6
 
-EDGES = (0, 6, 10, 14, 16)
+EDGES = (0, 4, 8, 14, 16)
+AHEAD = 2
 STEP = 2
 
 
@@ -21,7 +22,6 @@
 SMEM = pl.BlockSpec(memory_space=pltpu.SMEM)
 ANY = pl.BlockSpec(memory_space=pl.ANY)
 PARAMS = pltpu.CompilerParams(vmem_limit_bytes=25165824)
-WIDE = pltpu.CompilerParams(vmem_limit_bytes=60817408)
 ALONE = pltpu.CompilerParams(vmem_limit_bytes=67043328)
 
 
@@ -141,7 +141,7 @@
         out_specs=VMEM,
         out_shape=jax.ShapeDtypeStruct((2 * count, size, RQ * window), tentative.dtype),
         scratch_shapes=[pltpu.VMEM((3 * RQ + 1, size, window), tentative.dtype)] * (2 * step),
-        compiler_params=PARAMS if first else WIDE,
+        compiler_params=PARAMS,
         cost_estimate=cost(
             2 * count * per * (slots + 2) * size * size * window,
             2 * count * per * (slots + 7) * size * size,
@@ -436,7 +436,7 @@
         keep, send = coarse_rows(
             table, place, off_blocks, diag_blocks, field, near_a, near_b, low, columns
         )
-        if part == 0:
+        if part < AHEAD:
             other = lax.ppermute(send, "col", pair_a)
             total = (keep + other.astype(jnp.float32)).astype(link)
         else:
@@ -446,12 +446,18 @@
         parts.append((total, other))
 
     starts = [low for low, _ in spans]
-    keep, *send = split_groups(targets, place, None, parts[:1], starts[:1], rows)
+    keep, *send = split_groups(
+        targets, place, None, parts[:AHEAD], starts[:AHEAD], rows
+    )
     terms = exchange(keep, tuple(send), "row", rows, 2, link)
     blocks = sum(term[0].astype(jnp.float32) for term in terms)
     folded = exchange(blocks[0::2], blocks[1::2].astype(link), "col", columns, 2, link)
 
-    early = gather_groups(targets, place, parts[1:-2], starts[1:-2], rows)
+    early = None
+    if parts[AHEAD:-2]:
+        early = gather_groups(
+            targets, place, parts[AHEAD:-2], starts[AHEAD:-2], rows
+        )
     keep, *send = split_groups(targets, place, early, parts[-2:], starts[-2:], rows)
     return finish(*exchange(keep, tuple(send), "row", rows, 2, link), *folded)
 

time: 149 us -> 145 us (0.973)
  waiting for transfers between devices: 56.6 us -> 74.8 us
  local copies, waits for them, and re-layouts: 17.5 us -> 7.24 us
  Pallas kernels: 36.2 us -> 30.4 us
  starting transfers between devices: 34.7 us -> 29.5 us
    ppermute x9, waiting for transfers between devices: 29.3 us -> 46.5 us  [both(): near_b = lax.ppermute(block, 'col', pair_b)]
    unnamed x50 -> x24, local copies, waits for them, and re-layouts: 17.5 us -> 7.2 us
    ppermute x9, starting transfers between devices: 9.43 us -> 6.05 us  [both(): near_b = lax.ppermute(block, 'col', pair_b)]
    pallas_call x4, Pallas kernels: 14.3 us -> 11.3 us  [prolong_rows(): pl.pallas_call(functools.partial(prolong_kernel, first), grid=(count // s...]
    ppermute x4, starting transfers between devices: 7.04 us -> 4.31 us  [on_device(): other = lax.ppermute(total, 'row', flip(rows, 1))]
    ppermute x9 -> x7, waiting for transfers between devices: 7.04 us -> 9.09 us  [exchange(): arrived = (lax.ppermute(send, axis, route), 2)]
    ppermute x9 -> x7, starting transfers between devices: 8.39 us -> 8.09 us  [exchange(): arrived = (lax.ppermute(send, axis, route), 2)]
  transfers between devices with their start and end apart: 37 -> 36, of which waited for: 13 -> 12; matrix products, arithmetic and copies ran while one was open for 2% -> 1% of each run, Pallas kernels for 24% -> 19%
where the time goes in v1:
time: 145 us; the launch traced here: 144 us
  waiting for transfers between devices  74.8 us (52%)
  Pallas kernels  30.4 us (21%)
  starting transfers between devices  29.5 us (20%)
  local copies, waits for them, and re-layouts  7.24 us (5%)
  other arithmetic  2.06 us (1%)
    ppermute x9, waiting for transfers between devices, both(): near_b = lax.ppermute(block, 'col', pair_b)  46.5 us
    pallas_call x4, Pallas kernels, coarse_rows(): pl.pallas_call(functools.partial(coarse_kernel, first), grid=(count // st...  11.5 us
    pallas_call x4, Pallas kernels, prolong_rows(): pl.pallas_call(functools.partial(prolong_kernel, first), grid=(count // s...  11.3 us
    ppermute x7, waiting for transfers between devices, exchange(): arrived = (lax.ppermute(send, axis, route), 2)  9.09 us
    ppermute x2, waiting for transfers between devices, exchange(): odd = lax.ppermute(send[0], axis, route)  8.48 us
    ppermute x7, starting transfers between devices, exchange(): arrived = (lax.ppermute(send, axis, route), 2)  8.09 us
    unnamed x24, local copies, waits for them, and re-layouts  7.2 us
    ppermute x2, waiting for transfers between devices, exchange(): arrived = (lax.ppermute(send[1], axis, route), 1)  6.08 us
  transfers between devices with their start and end apart: 36, of which 12 were waited for; matrix products, arithmetic and copies ran while one was open for 1% of the time, Pallas kernels for 19%

profile of v1, /device:TPU:0, one launch (start us, length us, event | category | flops | bytes accessed | tf_op | source)
XLA Modules:
  0.0 144.3 jit_solution(12916678860886730732)
XLA Ops:
  0.0 2.4 %collective-permute-start.1 = (s32[64]{0:T(128)}, s32[64]{0:T(128)}, u32[]{:S(2)}, u32[]{:S(2)}) collective-permute-start(s32[64]{0:T(128)} %param.15), channel_id=1, source_target_pairs={{0,3},{1,2},{2,1},{3,0},{4,7},{5,6},{6,5},{7,4},{8,11},{9,10},{10,... | collective-permute-start | bytes 776 | tf_op jit(solution)/shard_map/ppermute | solution.py:410
  2.4 0.7 collective-permute-start
  3.1 1.9 %shard_map.97 = bf16[4,96,384]{2,1,0:T(8,128)(2,1)} custom-call(bf16[64,96,96]{2,1,0:T(8,128)(2,1)} %own.7), custom_call_target="tpu_custom_call" | custom-call | bytes 737280 | tf_op jit(solution)/shard_map/pallas_call | solution.py:55
  5.1 0.8 bitcast_add_fusion
  5.8 2.0 %collective-permute-start.2 = (s32[32]{0:T(128)S(1)}, s32[32]{0:T(128)S(1)}, u32[]{:S(2)}, u32[]{:S(2)}) collective-permute-start(s32[32]{0:T(128)S(1)} %bitcast_add_fusion), channel_id=1, source_target_pairs={{0,4},{4,0},{8,12},{12,8},{16,20},{20,16},{24,28},{28,24},{1,5},{5... | collective-permute-start | bytes 392 | tf_op jit(solution)/shard_map/ppermute | solution.py:420
  7.8 1.4 copy-done.2
  10.6 1.2 collective-permute-start.27
  11.8 0.7 pad_add_fusion.labels
  12.5 1.3 collective-permute-done.21.near_b
  13.9 2.8 %copy-done = bf16[64,4,96,96]{3,2,1,0:T(8,128)(2,1)S(1)} copy-done((bf16[64,4,96,96]{3,2,1,0:T(8,128)(2,1)S(1)}, bf16[64,4,96,96]{3,2,1,0:T(8,128)(2,1)}, u32[]{:S(2)}) %copy-start) | copy-done | bytes 4718616
  16.7 1.4 copy-done.3
  18.1 1.4 copy-done.5
  19.5 2.8 %shard_map.98.own = bf16[8,96,384]{2,1,0:T(8,128)(2,1)S(1)} custom-call(s32[4,64]{1,0:T(4,128)S(1)} %fusion.4.table, s32[3,64]{1,0:T(4,128)S(1)} %pad_add_fusion.labels, bf16[64,4,96,96]{3,2,1,0:T(8,128)(2,1)S(1)} %copy-done, bf16[64,96,96]{2,1,0:T(8,128)(2,1)S(1)} %copy-done.1, bf16[64,96,96]{2,1,0:T(8,128)(2,1)S(1)} %copy-done.5, ...), custom_call_target="tpu_custom_call" | custom-call | flops 339738624 | bytes 3244032 | tf_op jit(solution)/shard_map/pallas_call | solution.py:128
  22.3 1.6 %collective-permute-start.22 = (bf16[8,96,384]{2,1,0:T(8,128)(2,1)S(1)}, bf16[8,96,384]{2,1,0:T(8,128)(2,1)S(1)}, u32[]{:S(2)}, u32[]{:S(2)}) collective-permute-start(bf16[8,96,384]{2,1,0:T(8,128)(2,1)S(1)} %shard_map.98.own), channel_id=1, source_target_pairs={{0,1},{1,0},{2,3},{3,2},{4,5},{5,4},{6,7},{7,6},{8,9},{9,8},{10,11... | collective-permute-start | bytes 1769480 | tf_op jit(solution)/shard_map/ppermute | solution.py:411
  23.9 1.7 %collective-permute-start.4 = (bf16[6,96,384]{2,1,0:T(8,128)(2,1)S(1)}, bf16[6,96,384]{2,1,0:T(8,128)(2,1)S(1)}, u32[]{:S(2)}, u32[]{:S(2)}) collective-permute-start(bf16[6,96,384]{2,1,0:T(8,128)(2,1)S(1)} %get-tuple-element.30), channel_id=1, source_target_pairs={{0,3},{1,2},{2,1},{3,0},{4,7},{5,6},{6,5},{7,4},{8,11},{9,10},{10,... | collective-permute-start | bytes 1327112 | tf_op jit(solution)/shard_map/ppermute | solution.py:410
  25.6 2.8 %shard_map.100.own = bf16[8,96,384]{2,1,0:T(8,128)(2,1)S(1)} custom-call(s32[4,64]{1,0:T(4,128)S(1)} %fusion.4.table, s32[3,64]{1,0:T(4,128)S(1)} %pad_add_fusion.labels, bf16[64,4,96,96]{3,2,1,0:T(8,128)(2,1)S(1)} %copy-done, bf16[64,96,96]{2,1,0:T(8,128)(2,1)S(1)} %copy-done.1, bf16[64,96,96]{2,1,0:T(8,128)(2,1)S(1)} %copy-done.5, ...), custom_call_target="tpu_custom_call" | custom-call | flops 339738624 | bytes 3244032 | tf_op jit(solution)/shard_map/pallas_call | solution.py:128
  28.7 20.0 %collective-permute-done.4.near_b = bf16[6,96,384]{2,1,0:T(8,128)(2,1)S(1)} collective-permute-done((bf16[6,96,384]{2,1,0:T(8,128)(2,1)S(1)}, bf16[6,96,384]{2,1,0:T(8,128)(2,1)S(1)}, u32[]{:S(2)}, u32[]{:S(2)}) %collective-permute-start.4) | collective-permute-done | bytes 442400 | tf_op jit(solution)/shard_map/ppermute | solution.py:410
  48.7 3.9 %shard_map.92.own = bf16[12,96,384]{2,1,0:T(8,128)(2,1)S(1)} custom-call(s32[4,64]{1,0:T(4,128)S(1)} %fusion.4.table, s32[3,64]{1,0:T(4,128)S(1)} %pad_add_fusion.labels, bf16[64,4,96,96]{3,2,1,0:T(8,128)(2,1)S(1)} %copy-done, bf16[64,96,96]{2,1,0:T(8,128)(2,1)S(1)} %copy-done.1, bf16[64,96,96]{2,1,0:T(8,128)(2,1)S(1)} %copy-done.5, ...), custom_call_target="tpu_custom_call" | custom-call | flops 509607936 | bytes 4866048 | tf_op jit(solution)/shard_map/pallas_call | solution.py:128
  52.7 0.7 collective-permute-start.5
  53.4 2.9 %shard_map.99 = (f32[2,4,48,384]{3,2,1,0:T(8,128)S(1)}, bf16[2,4,48,384]{3,2,1,0:T(8,128)(2,1)S(1)}) custom-call(s32[4,64]{1,0:T(4,128)S(1)} %fusion.4.table, s32[2]{0:T(128)S(1)} %pad_add_fusion.2.place, bf16[64,4,96,96]{3,2,1,0:T(8,128)(2,1)S(1)} %bitcast.16, bf16[64,96,96]{2,1,0:T(8,128)(2,1)S(1)} %copy-done.1, bf16[8,96,384]{2,1,0:T(8,128)(2,1)S(1)} %shard_map.98.own, ...), custom_call_target="tpu_custom_call" | custom-call | flops 396361728 | bytes 4718592 | tf_op jit(solution)/shard_map/pallas_call | solution.py:209
  57.0 4.4 %collective-permute-done.29.near_b = bf16[8,96,384]{2,1,0:T(8,128)(2,1)S(1)} collective-permute-done((bf16[8,96,384]{2,1,0:T(8,128)(2,1)S(1)}, bf16[8,96,384]{2,1,0:T(8,128)(2,1)S(1)}, u32[]{:S(2)}, u32[]{:S(2)}) %collective-permute-start.29) | collective-permute-done | bytes 589856 | tf_op jit(solution)/shard_map/ppermute | solution.py:410
  61.9 2.9 %shard_map.101 = (f32[2,4,48,384]{3,2,1,0:T(8,128)S(1)}, bf16[2,4,48,384]{3,2,1,0:T(8,128)(2,1)S(1)}) custom-call(s32[4,64]{1,0:T(4,128)S(1)} %fusion.4.table, s32[2]{0:T(128)S(1)} %pad_add_fusion.2.place, bf16[64,4,96,96]{3,2,1,0:T(8,128)(2,1)S(1)} %bitcast.16, bf16[64,96,96]{2,1,0:T(8,128)(2,1)S(1)} %copy-done.1, bf16[8,96,384]{2,1,0:T(8,128)(2,1)S(1)} %shard_map.100.own, ...), custom_call_target="tpu_custom_call" | custom-call | flops 396361728 | bytes 4718592 | tf_op jit(solution)/shard_map/pallas_call | solution.py:209
  65.0 18.5 %collective-permute-done.11.near_b = bf16[2,96,384]{2,1,0:T(8,128)(2,1)S(1)} collective-permute-done((bf16[2,96,384]{2,1,0:T(8,128)(2,1)S(1)}, bf16[2,96,384]{2,1,0:T(8,128)(2,1)S(1)}, u32[]{:S(2)}, u32[]{:S(2)}) %collective-permute-start.11) | collective-permute-done | bytes 147488 | tf_op jit(solution)/shard_map/ppermute | solution.py:410
  83.5 1.7 %shard_map.94.own = bf16[4,96,384]{2,1,0:T(8,128)(2,1)S(1)} custom-call(s32[4,64]{1,0:T(4,128)S(1)} %fusion.4.table, s32[3,64]{1,0:T(4,128)S(1)} %pad_add_fusion.labels, bf16[64,4,96,96]{3,2,1,0:T(8,128)(2,1)S(1)} %bitcast.16, bf16[64,96,96]{2,1,0:T(8,128)(2,1)S(1)} %copy-done.1, bf16[64,96,96]{2,1,0:T(8,128)(2,1)S(1)} %copy-done.6, ...), custom_call_target="tpu_custom_call" | custom-call | flops 169869312 | bytes 1622016 | tf_op jit(solution)/shard_map/pallas_call | solution.py:128
  85.4 1.6 %collective-permute-start.25 = (bf16[2,4,48,384]{3,2,1,0:T(8,128)(2,1)S(1)}, bf16[2,4,48,384]{3,2,1,0:T(8,128)(2,1)S(1)}, u32[]{:S(2)}, u32[]{:S(2)}) collective-permute-start(bf16[2,4,48,384]{3,2,1,0:T(8,128)(2,1)S(1)} %add_convert_fusion.2.refs_0_), channel_id=1, source_target_pairs={{0,4},{4,0},{8,12},{12,8},{16,20},{20,16},{24,28},{28,24},{1,5},{5... | collective-permute-start | bytes 884744 | tf_op jit(solution)/shard_map/ppermute | solution.py:445
  87.1 0.6 collective-permute-start.31
  87.7 4.1 %shard_map.93 = (f32[2,6,48,384]{3,2,1,0:T(8,128)S(1)}, bf16[2,6,48,384]{3,2,1,0:T(8,128)(2,1)S(1)}) custom-call(s32[4,64]{1,0:T(4,128)S(1)} %fusion.4.table, s32[2]{0:T(128)S(1)} %pad_add_fusion.2.place, bf16[64,4,96,96]{3,2,1,0:T(8,128)(2,1)S(1)} %bitcast.16, bf16[64,96,96]{2,1,0:T(8,128)(2,1)S(1)} %copy-done.1, bf16[12,96,384]{2,1,0:T(8,128)(2,1)S(1)} %shard_map.92.own, ...), custom_call_target="tpu_custom_call" | custom-call | flops 594542592 | bytes 7077888 | tf_op jit(solution)/shard_map/pallas_call | solution.py:209
  91.8 2.2 %collective-permute-done.13.near_b = bf16[4,96,384]{2,1,0:T(8,128)(2,1)S(1)} collective-permute-done((bf16[4,96,384]{2,1,0:T(8,128)(2,1)S(1)}, bf16[4,96,384]{2,1,0:T(8,128)(2,1)S(1)}, u32[]{:S(2)}, u32[]{:S(2)}) %collective-permute-start.13) | collective-permute-done | bytes 294944 | tf_op jit(solution)/shard_map/ppermute | solution.py:410
  94.1 1.7 %shard_map.95 = (f32[2,2,48,384]{3,2,1,0:T(8,128)S(1)}, bf16[2,2,48,384]{3,2,1,0:T(8,128)(2,1)S(1)}) custom-call(s32[4,64]{1,0:T(4,128)S(1)} %fusion.4.table, s32[2]{0:T(128)S(1)} %pad_add_fusion.2.place, bf16[64,4,96,96]{3,2,1,0:T(8,128)(2,1)S(1)} %bitcast.16, bf16[64,96,96]{2,1,0:T(8,128)(2,1)S(1)} %copy-done.1, bf16[4,96,384]{2,1,0:T(8,128)(2,1)S(1)} %shard_map.94.own, ...), custom_call_target="tpu_custom_call" | custom-call | flops 198180864 | bytes 2359296 | tf_op jit(solution)/shard_map/pallas_call | solution.py:209
  95.8 0.8 collective-permute-start.14
  96.6 4.6 %collective-permute-done.31.refs_3_ = bf16[2,4,48,384]{3,2,1,0:T(8,128)(2,1)S(1)} collective-permute-done((bf16[2,4,48,384]{3,2,1,0:T(8,128)(2,1)S(1)}, bf16[2,4,48,384]{3,2,1,0:T(8,128)(2,1)S(1)}, u32[]{:S(2)}, u32[]{:S(2)}) %collective-permute-start.31) | collective-permute-done | bytes 294944 | tf_op jit(solution)/shard_map/ppermute | solution.py:445
  101.1 2.2 %shard_map.102 = (f32[2,2,4,48,384]{4,3,2,1,0:T(8,128)S(1)}, bf16[1,2,4,48,384]{4,3,2,1,0:T(8,128)(2,1)S(1)}, bf16[1,2,4,48,384]{4,3,2,1,0:T(8,128)(2,1)S(1)}) custom-call(s32[2,32]{1,0:T(2,128)S(1)} %pad_add_fusion.1.targets, s32[2]{0:T(128)S(1)} %pad_add_fusion.2.place, bf16[2,4,48,384]{3,2,1,0:T(8,128)(2,1)S(1)} %add_convert_fusion.2.refs_0_, ...), custom_call_target="tpu_custom_call" | custom-call | flops 589824 | bytes 14745600 | tf_op jit(solution)/shard_map/pallas_call | solution.py:327
  103.4 1.6 %collective-permute-start.33 = (bf16[1,2,4,48,384]{4,3,2,1,0:T(8,128)(2,1)S(1)}, bf16[1,2,4,48,384]{4,3,2,1,0:T(8,128)(2,1)S(1)}, u32[]{:S(2)}, u32[]{:S(2)}) collective-permute-start(bf16[1,2,4,48,384]{4,3,2,1,0:T(8,128)(2,1)S(1)} %get-tuple-element.46), channel_id=1, source_target_pairs={{0,8},{4,12},{8,0},{12,4},{16,24},{20,28},{24,16},{28,20},{1,9},{5... | collective-permute-start | bytes 884744 | tf_op jit(solution)/shard_map/ppermute | solution.py:372
  105.0 1.8 %collective-permute-start.15 = (bf16[1,2,48,384]{3,2,1,0:T(8,128)(2,1)S(1)}, bf16[1,2,48,384]{3,2,1,0:T(8,128)(2,1)S(1)}, u32[]{:S(2)}, u32[]{:S(2)}) collective-permute-start(bf16[1,2,48,384]{3,2,1,0:T(8,128)(2,1)S(1)} %add_convert_fusion.7), channel_id=1, source_target_pairs={{0,2},{1,3},{2,0},{3,1},{4,6},{5,7},{6,4},{7,5},{8,10},{9,11},{10,... | collective-permute-start | bytes 221192 | tf_op jit(solution)/shard_map/ppermute | solution.py:375
  107.7 5.6 %collective-permute-done.33 = bf16[1,2,4,48,384]{4,3,2,1,0:T(8,128)(2,1)S(1)} collective-permute-done((bf16[1,2,4,48,384]{4,3,2,1,0:T(8,128)(2,1)S(1)}, bf16[1,2,4,48,384]{4,3,2,1,0:T(8,128)(2,1)S(1)}, u32[]{:S(2)}, u32[]{:S(2)}) %collective-permute-start.33) | collective-permute-done | bytes 294944 | tf_op jit(solution)/shard_map/ppermute | solution.py:372
  113.4 2.6 %collective-permute-start.34 = (bf16[1,2,4,48,384]{4,3,2,1,0:T(8,128)(2,1)S(1)}, bf16[1,2,4,48,384]{4,3,2,1,0:T(8,128)(2,1)S(1)}, u32[]{:S(2)}, u32[]{:S(2)}) collective-permute-start(bf16[1,2,4,48,384]{4,3,2,1,0:T(8,128)(2,1)S(1)} %add_convert_fusion), channel_id=1, source_target_pairs={{0,16},{4,20},{8,24},{12,28},{16,0},{20,4},{24,8},{28,12},{1,17},{... | collective-permute-start | bytes 884744 | tf_op jit(solution)/shard_map/ppermute | solution.py:375
  116.1 1.6 %collective-permute-start.16 = (bf16[1,2,48,384]{3,2,1,0:T(8,128)(2,1)S(1)}, bf16[1,2,48,384]{3,2,1,0:T(8,128)(2,1)S(1)}, u32[]{:S(2)}, u32[]{:S(2)}) collective-permute-start(bf16[1,2,48,384]{3,2,1,0:T(8,128)(2,1)S(1)} %add_convert_fusion.6.refs_2_), channel_id=1, source_target_pairs={{0,4},{4,0},{8,12},{12,8},{16,20},{20,16},{24,28},{28,24},{1,5},{5... | collective-permute-start | bytes 221192 | tf_op jit(solution)/shard_map/ppermute | solution.py:445
  117.7 0.6 collective-permute-start.9
  118.3 5.5 %collective-permute-done.32 = bf16[1,2,4,48,384]{4,3,2,1,0:T(8,128)(2,1)S(1)} collective-permute-done((bf16[1,2,4,48,384]{4,3,2,1,0:T(8,128)(2,1)S(1)}, bf16[1,2,4,48,384]{4,3,2,1,0:T(8,128)(2,1)S(1)}, u32[]{:S(2)}, u32[]{:S(2)}) %collective-permute-start.32) | collective-permute-done | bytes 294944 | tf_op jit(solution)/shard_map/ppermute | solution.py:373
  123.8 3.6 %collective-permute-done.34 = bf16[1,2,4,48,384]{4,3,2,1,0:T(8,128)(2,1)S(1)} collective-permute-done((bf16[1,2,4,48,384]{4,3,2,1,0:T(8,128)(2,1)S(1)}, bf16[1,2,4,48,384]{4,3,2,1,0:T(8,128)(2,1)S(1)}, u32[]{:S(2)}, u32[]{:S(2)}) %collective-permute-start.34) | collective-permute-done | bytes 294944 | tf_op jit(solution)/shard_map/ppermute | solution.py:375
  127.5 2.1 %shard_map.96 = (f32[2,1,4,48,384]{4,3,2,1,0:T(8,128)S(1)}, bf16[1,1,4,48,384]{4,3,2,1,0:T(8,128)(2,1)S(1)}, bf16[1,1,4,48,384]{4,3,2,1,0:T(8,128)(2,1)S(1)}) custom-call(s32[2,32]{1,0:T(2,128)S(1)} %pad_add_fusion.1.targets, s32[2]{0:T(128)S(1)} %pad_add_fusion.2.place, bf16[1,6,48,384]{3,2,1,0:T(8,128)(2,1)S(1)} %add_convert_fusion.3.refs_0_, ...), custom_call_target="tpu_custom_call" | custom-call | flops 589824 | bytes 14745600 | tf_op jit(solution)/shard_map/pallas_call | solution.py:327
  129.9 1.5 %collective-permute-start.35 = (bf16[1,4,48,384]{3,2,1,0:T(8,128)(2,1)S(1)}, bf16[1,4,48,384]{3,2,1,0:T(8,128)(2,1)S(1)}, u32[]{:S(2)}, u32[]{:S(2)}) collective-permute-start(bf16[1,4,48,384]{3,2,1,0:T(8,128)(2,1)S(1)} %fusion), channel_id=1, source_target_pairs={{0,2},{1,3},{2,0},{3,1},{4,6},{5,7},{6,4},{7,5},{8,10},{9,11},{10,... | collective-permute-start | bytes 442376 | tf_op jit(solution)/shard_map/ppermute | solution.py:375
  131.5 2.0 %collective-permute-start.17 = (bf16[1,1,4,48,384]{4,3,2,1,0:T(8,128)(2,1)S(1)}, bf16[1,1,4,48,384]{4,3,2,1,0:T(8,128)(2,1)S(1)}, u32[]{:S(2)}, u32[]{:S(2)}) collective-permute-start(bf16[1,1,4,48,384]{4,3,2,1,0:T(8,128)(2,1)S(1)} %get-tuple-element.37), channel_id=1, source_target_pairs={{0,8},{4,12},{8,0},{12,4},{16,24},{20,28},{24,16},{28,20},{1,9},{5... | collective-permute-start | bytes 442376 | tf_op jit(solution)/shard_map/ppermute | solution.py:373
  133.5 2.9 %collective-permute-done.18 = bf16[1,1,4,48,384]{4,3,2,1,0:T(8,128)(2,1)S(1)} collective-permute-done((bf16[1,1,4,48,384]{4,3,2,1,0:T(8,128)(2,1)S(1)}, bf16[1,1,4,48,384]{4,3,2,1,0:T(8,128)(2,1)S(1)}, u32[]{:S(2)}, u32[]{:S(2)}) %collective-permute-start.18) | collective-permute-done | bytes 147488 | tf_op jit(solution)/shard_map/ppermute | solution.py:372
  136.4 0.9 collective-permute-start.19
  137.3 0.6 collective-permute-done.17.refs_1_
  137.9 5.5 %collective-permute-done.19.refs_2_ = bf16[1,1,4,48,384]{4,3,2,1,0:T(8,128)(2,1)S(1)} collective-permute-done((bf16[1,1,4,48,384]{4,3,2,1,0:T(8,128)(2,1)S(1)}, bf16[1,1,4,48,384]{4,3,2,1,0:T(8,128)(2,1)S(1)}, u32[]{:S(2)}, u32[]{:S(2)}) %collective-permute-start.19) | collective-permute-done | bytes 147488 | tf_op jit(solution)/shard_map/ppermute | solution.py:375
  143.4 0.9 shard_map.103
  (78 shorter events, 4.9 us)
Async XLA Ops:
  0.0 10.1 %collective-permute-start.1 = (s32[64]{0:T(128)}, s32[64]{0:T(128)}, u32[]{:S(2)}, u32[]{:S(2)}) collective-permute-start(s32[64]{0:T(128)} %param.15), channel_id=1, source_target_pairs={{0,3},{1,2},{2,1},{3,0},{4,7},{5,6},{6,5},{7,4},{8,11},{9,10},{10,... | collective-permute-start | bytes 776 | tf_op jit(solution)/shard_map/ppermute | solution.py:410
  2.4 8.2 %collective-permute-start = (s32[64]{0:T(128)}, s32[64]{0:T(128)}, u32[]{:S(2)}, u32[]{:S(2)}) collective-permute-start(s32[64]{0:T(128)} %param.15), channel_id=1, source_target_pairs={{0,1},{1,0},{2,3},{3,2},{4,5},{5,4},{6,7},{7,6},{8,9},{9,8},{10,11... | collective-permute-start | bytes 776 | tf_op jit(solution)/shard_map/ppermute | solution.py:411
  5.0 8.8 %copy-start.1 = (bf16[64,96,96]{2,1,0:T(8,128)(2,1)S(1)}, bf16[64,96,96]{2,1,0:T(8,128)(2,1)}, u32[]{:S(2)}) copy-start(bf16[64,96,96]{2,1,0:T(8,128)(2,1)} %diag.15) | copy-start | bytes 3538948
  5.0 7.5 %collective-permute-start.20 = (bf16[4,96,384]{2,1,0:T(8,128)(2,1)}, bf16[4,96,384]{2,1,0:T(8,128)(2,1)S(1)}, u32[]{:S(2)}, u32[]{:S(2)}) collective-permute-start(bf16[4,96,384]{2,1,0:T(8,128)(2,1)} %shard_map.97), channel_id=1, source_target_pairs={{0,1},{1,0},{2,3},{3,2},{4,5},{5,4},{6,7},{7,6},{8,9},{9,8},{10,11... | collective-permute-start | bytes 884744 | tf_op jit(solution)/shard_map/ppermute | solution.py:411
  5.0 8.8 %collective-permute-start.21 = (bf16[4,96,384]{2,1,0:T(8,128)(2,1)}, bf16[4,96,384]{2,1,0:T(8,128)(2,1)S(1)}, u32[]{:S(2)}, u32[]{:S(2)}) collective-permute-start(bf16[4,96,384]{2,1,0:T(8,128)(2,1)} %shard_map.97), channel_id=1, source_target_pairs={{0,3},{1,2},{2,1},{3,0},{4,7},{5,6},{6,5},{7,4},{8,11},{9,10},{10,... | collective-permute-start | bytes 884744 | tf_op jit(solution)/shard_map/ppermute | solution.py:410
  5.8 4.1 %collective-permute-start.2 = (s32[32]{0:T(128)S(1)}, s32[32]{0:T(128)S(1)}, u32[]{:S(2)}, u32[]{:S(2)}) collective-permute-start(s32[32]{0:T(128)S(1)} %bitcast_add_fusion), channel_id=1, source_target_pairs={{0,4},{4,0},{8,12},{12,8},{16,20},{20,16},{24,28},{28,24},{1,5},{5... | collective-permute-start | bytes 392 | tf_op jit(solution)/shard_map/ppermute | solution.py:420
  7.8 1.4 copy-start.2
  9.2 0.7 copy-start.7
  9.2 0.7 copy-start.8
  9.2 2.6 %copy-start.9 = (s32[64]{0:T(128)S(1)}, s32[64]{0:T(128)}, u32[]{:S(2)}) copy-start(s32[64]{0:T(128)} %param.15) | copy-start | bytes 772
  10.0 18.7 %collective-permute-start.3 = (bf16[6,96,384]{2,1,0:T(8,128)(2,1)S(1)}, bf16[6,96,384]{2,1,0:T(8,128)(2,1)S(1)}, u32[]{:S(2)}, u32[]{:S(2)}) collective-permute-start(bf16[6,96,384]{2,1,0:T(8,128)(2,1)S(1)} %get-tuple-element.30), channel_id=1, source_target_pairs={{0,1},{1,0},{2,3},{3,2},{4,5},{5,4},{6,7},{7,6},{8,9},{9,8},{10,11... | collective-permute-start | bytes 1327112 | tf_op jit(solution)/shard_map/ppermute | solution.py:411
  10.1 13.8 %collective-permute-start.26 = (bf16[4,96,384]{2,1,0:T(8,128)(2,1)S(1)}, bf16[4,96,384]{2,1,0:T(8,128)(2,1)S(1)}, u32[]{:S(2)}, u32[]{:S(2)}) collective-permute-start(bf16[4,96,384]{2,1,0:T(8,128)(2,1)S(1)} %get-tuple-element.41), channel_id=1, source_target_pairs={{0,1},{1,0},{2,3},{3,2},{4,5},{5,4},{6,7},{7,6},{8,9},{9,8},{10,11... | collective-permute-start | bytes 884744 | tf_op jit(solution)/shard_map/ppermute | solution.py:411
  10.6 15.0 %collective-permute-start.27 = (bf16[4,96,384]{2,1,0:T(8,128)(2,1)S(1)}, bf16[4,96,384]{2,1,0:T(8,128)(2,1)S(1)}, u32[]{:S(2)}, u32[]{:S(2)}) collective-permute-start(bf16[4,96,384]{2,1,0:T(8,128)(2,1)S(1)} %get-tuple-element.41), channel_id=1, source_target_pairs={{0,3},{1,2},{2,1},{3,0},{4,7},{5,6},{6,5},{7,4},{8,11},{9,10},{10,... | collective-permute-start | bytes 884744 | tf_op jit(solution)/shard_map/ppermute | solution.py:410
  13.9 2.8 %copy-start = (bf16[64,4,96,96]{3,2,1,0:T(8,128)(2,1)S(1)}, bf16[64,4,96,96]{3,2,1,0:T(8,128)(2,1)}, u32[]{:S(2)}) copy-start(bf16[64,4,96,96]{3,2,1,0:T(8,128)(2,1)} %off.15) | copy-start | bytes 14155780
  16.7 1.4 copy-start.3
  18.1 1.4 copy-start.5
  22.3 31.1 %collective-permute-start.22 = (bf16[8,96,384]{2,1,0:T(8,128)(2,1)S(1)}, bf16[8,96,384]{2,1,0:T(8,128)(2,1)S(1)}, u32[]{:S(2)}, u32[]{:S(2)}) collective-permute-start(bf16[8,96,384]{2,1,0:T(8,128)(2,1)S(1)} %shard_map.98.own), channel_id=1, source_target_pairs={{0,1},{1,0},{2,3},{3,2},{4,5},{5,4},{6,7},{7,6},{8,9},{9,8},{10,11... | collective-permute-start | bytes 1769480 | tf_op jit(solution)/shard_map/ppermute | solution.py:411
  23.9 29.5 %collective-permute-start.23 = (bf16[8,96,384]{2,1,0:T(8,128)(2,1)S(1)}, bf16[8,96,384]{2,1,0:T(8,128)(2,1)S(1)}, u32[]{:S(2)}, u32[]{:S(2)}) collective-permute-start(bf16[8,96,384]{2,1,0:T(8,128)(2,1)S(1)} %shard_map.98.own), channel_id=1, source_target_pairs={{0,3},{1,2},{2,1},{3,0},{4,7},{5,6},{6,5},{7,4},{8,11},{9,10},{10,... | collective-permute-start | bytes 1769480 | tf_op jit(solution)/shard_map/ppermute | solution.py:410
  23.9 24.8 %collective-permute-start.4 = (bf16[6,96,384]{2,1,0:T(8,128)(2,1)S(1)}, bf16[6,96,384]{2,1,0:T(8,128)(2,1)S(1)}, u32[]{:S(2)}, u32[]{:S(2)}) collective-permute-start(bf16[6,96,384]{2,1,0:T(8,128)(2,1)S(1)} %get-tuple-element.30), channel_id=1, source_target_pairs={{0,3},{1,2},{2,1},{3,0},{4,7},{5,6},{6,5},{7,4},{8,11},{9,10},{10,... | collective-permute-start | bytes 1327112 | tf_op jit(solution)/shard_map/ppermute | solution.py:410
  25.6 27.7 %slice-start = ((s8[6291456]{0:T(1024)(128)(4,1)}), s8[4194304]{0:T(1024)(128)(4,1)S(1)}, s32[]{:S(2)}) async-start(s8[6291456]{0:T(1024)(128)(4,1)} %bitcast.15), calls=%async_computation | async-start | bytes 8388608
  28.5 24.9 %slice-start.1 = ((s8[6291456]{0:T(1024)(128)(4,1)}), s8[2097152]{0:T(1024)(128)(4,1)S(1)}, s32[]{:S(2)}) async-start(s8[6291456]{0:T(1024)(128)(4,1)} %bitcast.15), calls=%async_computation.1 | async-start | bytes 4194304
  28.5 28.3 %collective-permute-start.28 = (bf16[8,96,384]{2,1,0:T(8,128)(2,1)S(1)}, bf16[8,96,384]{2,1,0:T(8,128)(2,1)S(1)}, u32[]{:S(2)}, u32[]{:S(2)}) collective-permute-start(bf16[8,96,384]{2,1,0:T(8,128)(2,1)S(1)} %shard_map.100.own), channel_id=1, source_target_pairs={{0,1},{1,0},{2,3},{3,2},{4,5},{5,4},{6,7},{7,6},{8,9},{9,8},{10,11... | collective-permute-start | bytes 1769480 | tf_op jit(solution)/shard_map/ppermute | solution.py:411
  28.6 32.7 %collective-permute-start.29 = (bf16[8,96,384]{2,1,0:T(8,128)(2,1)S(1)}, bf16[8,96,384]{2,1,0:T(8,128)(2,1)S(1)}, u32[]{:S(2)}, u32[]{:S(2)}) collective-permute-start(bf16[8,96,384]{2,1,0:T(8,128)(2,1)S(1)} %shard_map.100.own), channel_id=1, source_target_pairs={{0,3},{1,2},{2,1},{3,0},{4,7},{5,6},{6,5},{7,4},{8,11},{9,10},{10,... | collective-permute-start | bytes 1769480 | tf_op jit(solution)/shard_map/ppermute | solution.py:410
  52.7 34.4 %collective-permute-start.5 = (bf16[12,96,384]{2,1,0:T(8,128)(2,1)S(1)}, bf16[12,96,384]{2,1,0:T(8,128)(2,1)S(1)}, u32[]{:S(2)}, u32[]{:S(2)}) collective-permute-start(bf16[12,96,384]{2,1,0:T(8,128)(2,1)S(1)} %shard_map.92.own), channel_id=1, source_target_pairs={{0,1},{1,0},{2,3},{3,2},{4,5},{5,4},{6,7},{7,6},{8,9},{9,8},{10,11... | collective-permute-start | bytes 2654216 | tf_op jit(solution)/shard_map/ppermute | solution.py:411
  53.4 34.3 %collective-permute-start.6 = (bf16[12,96,384]{2,1,0:T(8,128)(2,1)S(1)}, bf16[12,96,384]{2,1,0:T(8,128)(2,1)S(1)}, u32[]{:S(2)}, u32[]{:S(2)}) collective-permute-start(bf16[12,96,384]{2,1,0:T(8,128)(2,1)S(1)} %shard_map.92.own), channel_id=1, source_target_pairs={{0,3},{1,2},{2,1},{3,0},{4,7},{5,6},{6,5},{7,4},{8,11},{9,10},{10,... | collective-permute-start | bytes 2654216 | tf_op jit(solution)/shard_map/ppermute | solution.py:410
  56.3 29.0 %collective-permute-start.24 = (bf16[2,4,48,384]{3,2,1,0:T(8,128)(2,1)S(1)}, bf16[2,4,48,384]{3,2,1,0:T(8,128)(2,1)S(1)}, u32[]{:S(2)}, u32[]{:S(2)}) collective-permute-start(bf16[2,4,48,384]{3,2,1,0:T(8,128)(2,1)S(1)} %get-tuple-element.40), channel_id=1, source_target_pairs={{0,1},{1,0},{2,3},{3,2},{4,5},{5,4},{6,7},{7,6},{8,9},{9,8},{10,11... | collective-permute-start | bytes 884744 | tf_op jit(solution)/shard_map/ppermute | solution.py:440
  56.8 26.7 %copy-start.4 = (bf16[64,96,96]{2,1,0:T(8,128)(2,1)S(1)}, bf16[64,96,96]{2,1,0:T(8,128)(2,1)}, u32[]{:S(2)}) copy-start(bf16[64,96,96]{2,1,0:T(8,128)(2,1)} %own.7) | copy-start | bytes 3538948
  56.8 26.7 %copy-start.6 = (bf16[64,96,96]{2,1,0:T(8,128)(2,1)S(1)}, bf16[64,96,96]{2,1,0:T(8,128)(2,1)}, u32[]{:S(2)}) copy-start(bf16[64,96,96]{2,1,0:T(8,128)(2,1)} %inverse.7) | copy-start | bytes 3538948
  56.8 8.0 %collective-permute-start.10 = (bf16[2,96,384]{2,1,0:T(8,128)(2,1)S(1)}, bf16[2,96,384]{2,1,0:T(8,128)(2,1)S(1)}, u32[]{:S(2)}, u32[]{:S(2)}) collective-permute-start(bf16[2,96,384]{2,1,0:T(8,128)(2,1)S(1)} %get-tuple-element.33), channel_id=1, source_target_pairs={{0,1},{1,0},{2,3},{3,2},{4,5},{5,4},{6,7},{7,6},{8,9},{9,8},{10,11... | collective-permute-start | bytes 442376 | tf_op jit(solution)/shard_map/ppermute | solution.py:411
  61.4 22.1 %collective-permute-start.11 = (bf16[2,96,384]{2,1,0:T(8,128)(2,1)S(1)}, bf16[2,96,384]{2,1,0:T(8,128)(2,1)S(1)}, u32[]{:S(2)}, u32[]{:S(2)}) collective-permute-start(bf16[2,96,384]{2,1,0:T(8,128)(2,1)S(1)} %get-tuple-element.33), channel_id=1, source_target_pairs={{0,3},{1,2},{2,1},{3,0},{4,7},{5,6},{6,5},{7,4},{8,11},{9,10},{10,... | collective-permute-start | bytes 442376 | tf_op jit(solution)/shard_map/ppermute | solution.py:410
  64.8 20.6 %collective-permute-start.30 = (bf16[2,4,48,384]{3,2,1,0:T(8,128)(2,1)S(1)}, bf16[2,4,48,384]{3,2,1,0:T(8,128)(2,1)S(1)}, u32[]{:S(2)}, u32[]{:S(2)}) collective-permute-start(bf16[2,4,48,384]{3,2,1,0:T(8,128)(2,1)S(1)} %get-tuple-element.43), channel_id=1, source_target_pairs={{0,1},{1,0},{2,3},{3,2},{4,5},{5,4},{6,7},{7,6},{8,9},{9,8},{10,11... | collective-permute-start | bytes 884744 | tf_op jit(solution)/shard_map/ppermute | solution.py:440
  85.2 6.7 %collective-permute-start.12 = (bf16[4,96,384]{2,1,0:T(8,128)(2,1)S(1)}, bf16[4,96,384]{2,1,0:T(8,128)(2,1)S(1)}, u32[]{:S(2)}, u32[]{:S(2)}) collective-permute-start(bf16[4,96,384]{2,1,0:T(8,128)(2,1)S(1)} %shard_map.94.own), channel_id=1, source_target_pairs={{0,1},{1,0},{2,3},{3,2},{4,5},{5,4},{6,7},{7,6},{8,9},{9,8},{10,11... | collective-permute-start | bytes 884744 | tf_op jit(solution)/shard_map/ppermute | solution.py:411
  85.4 8.7 %collective-permute-start.13 = (bf16[4,96,384]{2,1,0:T(8,128)(2,1)S(1)}, bf16[4,96,384]{2,1,0:T(8,128)(2,1)S(1)}, u32[]{:S(2)}, u32[]{:S(2)}) collective-permute-start(bf16[4,96,384]{2,1,0:T(8,128)(2,1)S(1)} %shard_map.94.own), channel_id=1, source_target_pairs={{0,3},{1,2},{2,1},{3,0},{4,7},{5,6},{6,5},{7,4},{8,11},{9,10},{10,... | collective-permute-start | bytes 884744 | tf_op jit(solution)/shard_map/ppermute | solution.py:410
  85.4 11.1 %collective-permute-start.25 = (bf16[2,4,48,384]{3,2,1,0:T(8,128)(2,1)S(1)}, bf16[2,4,48,384]{3,2,1,0:T(8,128)(2,1)S(1)}, u32[]{:S(2)}, u32[]{:S(2)}) collective-permute-start(bf16[2,4,48,384]{3,2,1,0:T(8,128)(2,1)S(1)} %add_convert_fusion.2.refs_0_), channel_id=1, source_target_pairs={{0,4},{4,0},{8,12},{12,8},{16,20},{20,16},{24,28},{28,24},{1,5},{5... | collective-permute-start | bytes 884744 | tf_op jit(solution)/shard_map/ppermute | solution.py:445
  87.1 14.1 %collective-permute-start.31 = (bf16[2,4,48,384]{3,2,1,0:T(8,128)(2,1)S(1)}, bf16[2,4,48,384]{3,2,1,0:T(8,128)(2,1)S(1)}, u32[]{:S(2)}, u32[]{:S(2)}) collective-permute-start(bf16[2,4,48,384]{3,2,1,0:T(8,128)(2,1)S(1)} %add_convert_fusion.1.refs_2_), channel_id=1, source_target_pairs={{0,4},{4,0},{8,12},{12,8},{16,20},{20,16},{24,28},{28,24},{1,5},{5... | collective-permute-start | bytes 884744 | tf_op jit(solution)/shard_map/ppermute | solution.py:445
  91.8 15.5 %collective-permute-start.7 = (bf16[2,6,48,384]{3,2,1,0:T(8,128)(2,1)S(1)}, bf16[2,6,48,384]{3,2,1,0:T(8,128)(2,1)S(1)}, u32[]{:S(2)}, u32[]{:S(2)}) collective-permute-start(bf16[2,6,48,384]{3,2,1,0:T(8,128)(2,1)S(1)} %get-tuple-element.32), channel_id=1, source_target_pairs={{0,1},{1,0},{2,3},{3,2},{4,5},{5,4},{6,7},{7,6},{8,9},{9,8},{10,11... | collective-permute-start | bytes 1327112 | tf_op jit(solution)/shard_map/ppermute | solution.py:375
  95.8 9.2 %collective-permute-start.14 = (bf16[2,2,48,384]{3,2,1,0:T(8,128)(2,1)S(1)}, bf16[2,2,48,384]{3,2,1,0:T(8,128)(2,1)S(1)}, u32[]{:S(2)}, u32[]{:S(2)}) collective-permute-start(bf16[2,2,48,384]{3,2,1,0:T(8,128)(2,1)S(1)} %get-tuple-element.35), channel_id=1, source_target_pairs={{0,1},{1,0},{2,3},{3,2},{4,5},{5,4},{6,7},{7,6},{8,9},{9,8},{10,11... | collective-permute-start | bytes 442376 | tf_op jit(solution)/shard_map/ppermute | solution.py:375
  103.4 9.9 %collective-permute-start.33 = (bf16[1,2,4,48,384]{4,3,2,1,0:T(8,128)(2,1)S(1)}, bf16[1,2,4,48,384]{4,3,2,1,0:T(8,128)(2,1)S(1)}, u32[]{:S(2)}, u32[]{:S(2)}) collective-permute-start(bf16[1,2,4,48,384]{4,3,2,1,0:T(8,128)(2,1)S(1)} %get-tuple-element.46), channel_id=1, source_target_pairs={{0,8},{4,12},{8,0},{12,4},{16,24},{20,28},{24,16},{28,20},{1,9},{5... | collective-permute-start | bytes 884744 | tf_op jit(solution)/shard_map/ppermute | solution.py:372
  105.0 11.0 %collective-permute-start.15 = (bf16[1,2,48,384]{3,2,1,0:T(8,128)(2,1)S(1)}, bf16[1,2,48,384]{3,2,1,0:T(8,128)(2,1)S(1)}, u32[]{:S(2)}, u32[]{:S(2)}) collective-permute-start(bf16[1,2,48,384]{3,2,1,0:T(8,128)(2,1)S(1)} %add_convert_fusion.7), channel_id=1, source_target_pairs={{0,2},{1,3},{2,0},{3,1},{4,6},{5,7},{6,4},{7,5},{8,10},{9,11},{10,... | collective-permute-start | bytes 221192 | tf_op jit(solution)/shard_map/ppermute | solution.py:375
  106.8 16.9 %collective-permute-start.32 = (bf16[1,2,4,48,384]{4,3,2,1,0:T(8,128)(2,1)S(1)}, bf16[1,2,4,48,384]{4,3,2,1,0:T(8,128)(2,1)S(1)}, u32[]{:S(2)}, u32[]{:S(2)}) collective-permute-start(bf16[1,2,4,48,384]{4,3,2,1,0:T(8,128)(2,1)S(1)} %get-tuple-element.45), channel_id=1, source_target_pairs={{0,8},{4,12},{8,0},{12,4},{16,24},{20,28},{24,16},{28,20},{1,9},{5... | collective-permute-start | bytes 884744 | tf_op jit(solution)/shard_map/ppermute | solution.py:373
  107.3 10.3 %collective-permute-start.8 = (bf16[1,6,48,384]{3,2,1,0:T(8,128)(2,1)S(1)}, bf16[1,6,48,384]{3,2,1,0:T(8,128)(2,1)S(1)}, u32[]{:S(2)}, u32[]{:S(2)}) collective-permute-start(bf16[1,6,48,384]{3,2,1,0:T(8,128)(2,1)S(1)} %add_convert_fusion.4), channel_id=1, source_target_pairs={{0,2},{1,3},{2,0},{3,1},{4,6},{5,7},{6,4},{7,5},{8,10},{9,11},{10,... | collective-permute-start | bytes 663560 | tf_op jit(solution)/shard_map/ppermute | solution.py:375
  113.4 14.0 %collective-permute-start.34 = (bf16[1,2,4,48,384]{4,3,2,1,0:T(8,128)(2,1)S(1)}, bf16[1,2,4,48,384]{4,3,2,1,0:T(8,128)(2,1)S(1)}, u32[]{:S(2)}, u32[]{:S(2)}) collective-permute-start(bf16[1,2,4,48,384]{4,3,2,1,0:T(8,128)(2,1)S(1)} %add_convert_fusion), channel_id=1, source_target_pairs={{0,16},{4,20},{8,24},{12,28},{16,0},{20,4},{24,8},{28,12},{1,17},{... | collective-permute-start | bytes 884744 | tf_op jit(solution)/shard_map/ppermute | solution.py:375
  116.1 11.4 %collective-permute-start.16 = (bf16[1,2,48,384]{3,2,1,0:T(8,128)(2,1)S(1)}, bf16[1,2,48,384]{3,2,1,0:T(8,128)(2,1)S(1)}, u32[]{:S(2)}, u32[]{:S(2)}) collective-permute-start(bf16[1,2,48,384]{3,2,1,0:T(8,128)(2,1)S(1)} %add_convert_fusion.6.refs_2_), channel_id=1, source_target_pairs={{0,4},{4,0},{8,12},{12,8},{16,20},{20,16},{24,28},{28,24},{1,5},{5... | collective-permute-start | bytes 221192 | tf_op jit(solution)/shard_map/ppermute | solution.py:445
  117.7 9.8 %collective-permute-start.9 = (bf16[1,6,48,384]{3,2,1,0:T(8,128)(2,1)S(1)}, bf16[1,6,48,384]{3,2,1,0:T(8,128)(2,1)S(1)}, u32[]{:S(2)}, u32[]{:S(2)}) collective-permute-start(bf16[1,6,48,384]{3,2,1,0:T(8,128)(2,1)S(1)} %add_convert_fusion.3.refs_0_), channel_id=1, source_target_pairs={{0,4},{4,0},{8,12},{12,8},{16,20},{20,16},{24,28},{28,24},{1,5},{5... | collective-permute-start | bytes 663560 | tf_op jit(solution)/shard_map/ppermute | solution.py:445
  129.6 6.8 %collective-permute-start.18 = (bf16[1,1,4,48,384]{4,3,2,1,0:T(8,128)(2,1)S(1)}, bf16[1,1,4,48,384]{4,3,2,1,0:T(8,128)(2,1)S(1)}, u32[]{:S(2)}, u32[]{:S(2)}) collective-permute-start(bf16[1,1,4,48,384]{4,3,2,1,0:T(8,128)(2,1)S(1)} %get-tuple-element.38), channel_id=1, source_target_pairs={{0,8},{4,12},{8,0},{12,4},{16,24},{20,28},{24,16},{28,20},{1,9},{5... | collective-permute-start | bytes 442376 | tf_op jit(solution)/shard_map/ppermute | solution.py:372
  129.9 7.4 %collective-permute-start.35 = (bf16[1,4,48,384]{3,2,1,0:T(8,128)(2,1)S(1)}, bf16[1,4,48,384]{3,2,1,0:T(8,128)(2,1)S(1)}, u32[]{:S(2)}, u32[]{:S(2)}) collective-permute-start(bf16[1,4,48,384]{3,2,1,0:T(8,128)(2,1)S(1)} %fusion), channel_id=1, source_target_pairs={{0,2},{1,3},{2,0},{3,1},{4,6},{5,7},{6,4},{7,5},{8,10},{9,11},{10,... | collective-permute-start | bytes 442376 | tf_op jit(solution)/shard_map/ppermute | solution.py:375
  131.5 6.5 %collective-permute-start.17 = (bf16[1,1,4,48,384]{4,3,2,1,0:T(8,128)(2,1)S(1)}, bf16[1,1,4,48,384]{4,3,2,1,0:T(8,128)(2,1)S(1)}, u32[]{:S(2)}, u32[]{:S(2)}) collective-permute-start(bf16[1,1,4,48,384]{4,3,2,1,0:T(8,128)(2,1)S(1)} %get-tuple-element.37), channel_id=1, source_target_pairs={{0,8},{4,12},{8,0},{12,4},{16,24},{20,28},{24,16},{28,20},{1,9},{5... | collective-permute-start | bytes 442376 | tf_op jit(solution)/shard_map/ppermute | solution.py:373
  136.4 7.0 %collective-permute-start.19 = (bf16[1,1,4,48,384]{4,3,2,1,0:T(8,128)(2,1)S(1)}, bf16[1,1,4,48,384]{4,3,2,1,0:T(8,128)(2,1)S(1)}, u32[]{:S(2)}, u32[]{:S(2)}) collective-permute-start(bf16[1,1,4,48,384]{4,3,2,1,0:T(8,128)(2,1)S(1)} %add_convert_fusion.5), channel_id=1, source_target_pairs={{0,16},{4,20},{8,24},{12,28},{16,0},{20,4},{24,8},{28,12},{1,17},{... | collective-permute-start | bytes 442376 | tf_op jit(solution)/shard_map/ppermute | solution.py:375
